TPU v7x, 256 devices: a whole 4x4x8 slice. The times are simulated.
256 devices in a mesh: freq: 32 (over y, z), pencil: 8 (over x, core).
Axes of the slice: x: 4, y: 4, z: 8, core: 2. Of those that a mesh axis runs over, the one named last changes fastest.
Arguments:
- wave_field: float32 [64, 512, 2, 512], P('freq', 'pencil'), may hold values from -6 to 6
- source_field: float32 [1, 64, 512, 2, 512], P(None, 'freq', 'pencil'), may hold values from -6 to 6
- omegas: float32 [64], P('freq'), may hold values from 30 to 250
- velocities: float32 [1, 6], replicated, may hold values from 1500 to 4500
- lower_ref: int32 [1, 8, 8], replicated, may hold values from 0 to 4, as said below
- blend_weight: float32 [1, 8, 8], replicated, may hold values from 0 to 1
Outputs:
- new_field: float32 [64, 512, 2, 512], P('freq', 'pencil')
- image: float32 [1, 512, 512], P(None, 'pencil', 'freq')
Inputs may be any that keep to these rules, and one draw needn't show every extreme that they name: `lower_ref`: in each depth step the lower references of one tile row differ by at most one, so a tile row's tiles use at most three consecutive references; in each depth step one tile row uses references 0 to 2 and another references 6 - 3 to 5.
All inputs are finite; a program needn't handle non-finite values.
Results may differ from a plain program's by a relative error of at most 0.0001.
Values sent between devices are 32-bit elements; how exact they have to be, the bound alone decides.
No kernel may reach another device: no remote copies, remote signals or barrier semaphores. Data moves between devices by JAX's collectives and lax.ppermute only.
A program may use at most 128 MiB of HBM per device.

v0:
```python
import functools
import math

import jax
import jax.numpy as jnp
import numpy as np
from jax import lax
from jax.experimental import pallas as pl
from jax.experimental.pallas import tpu as pltpu
from jax.sharding import PartitionSpec as P


N = 512
NREF = 6
NEED = 3
STEP = 10.0
UNIT = 2.0 * math.pi / (N * 12.5)
HALF = N // 2
QUART = N // 4
SLOTS = ((2, 0), (2, 1), (1, 0), (1, 1), (3, 0), (3, 1), (0, 1), (0, 0))
BF = jnp.bfloat16
F32 = jnp.float32
INTERPRET = False


def split(values):
    high = values.astype(BF)
    return high, (values - high.astype(F32)).astype(BF)


def tables():
    place = np.arange(HALF)
    cas = lambda k: (lambda t: np.cos(t) + np.sin(t))((place[:, None] * k[None, :] % N) * (2.0 * np.pi / N)) / np.sqrt(N)
    even, odd = cas(2 * place), cas(2 * place + 1)
    j = np.arange(QUART)
    fold_even = cas(np.concatenate([2 * j, [HALF], N - 2 * j[1:]]))
    fold_odd = cas(np.concatenate([2 * j + 1, N - 1 - 2 * j]))
    out = []
    for table in (even, odd, odd.T, fold_even.T, fold_odd.T, fold_even, fold_odd):
        high = np.asarray(table, np.float32).astype(jnp.bfloat16)
        low = (table - high.astype(np.float64)).astype(np.float32).astype(jnp.bfloat16)
        out.append(np.stack([high, low]))
    return out


def cat_left(pair):
    high, low = pair
    return jnp.concatenate([high, high, low], axis=1)


def cat_right(pair):
    high, low = pair
    return jnp.concatenate([high, low, high], axis=0)


def dot3(left, right):
    return jnp.dot(cat_left(left), cat_right(right), preferred_element_type=F32)


def both(ref):
    return ref[0], ref[1]


def low_lanes(shape):
    return lax.broadcasted_iota(jnp.int32, shape, len(shape) - 1) < 64


def forward_y(wave_ref, even_ref, odd_ref, out_ref):
    rows = jnp.concatenate([wave_ref[f, :, c, :] for f in range(2) for c in range(2)], axis=0)
    near, far = rows[:, :HALF], rows[:, HALF:]
    first = low_lanes((64, 128))
    for kind, (mixed, ref) in enumerate(((near + far, even_ref), (near - far, odd_ref))):
        spectrum = dot3(split(mixed), both(ref))
        for f in range(2):
            for m in range(2):
                lanes = slice(128 * m, 128 * m + 128)
                re = spectrum[128 * f : 128 * f + 64, lanes]
                im = spectrum[128 * f + 64 : 128 * f + 128, lanes]
                out_ref[4 * kind + 2 * m, f] = jnp.where(first, re, pltpu.roll(im, 64, 1))
                out_ref[4 * kind + 2 * m + 1, f] = jnp.where(first, pltpu.roll(re, 64, 1), im)


def phase_of(q):
    root = jnp.sqrt(jnp.abs(q)) * STEP
    u = jnp.maximum(q, 0.0) * (STEP * STEP)
    cosine = jnp.full_like(u, 1.0 / math.factorial(16))
    for k in range(7, -1, -1):
        cosine = cosine * u + (-1.0) ** k / math.factorial(2 * k)
    sine = jnp.full_like(u, -1.0 / math.factorial(15))
    for k in range(6, -1, -1):
        sine = sine * u + (-1.0) ** k / math.factorial(2 * k + 1)
    damping = jnp.exp(-root)
    moving = q > 0.0
    return jnp.where(moving, cosine, damping), jnp.where(moving, sine * root, 0.0)


def phases(pos_ref, omega_ref, speed_ref, cos_ref, sin_ref, nyq_ref):
    lane = lax.broadcasted_iota(jnp.int32, (QUART, 128), 1)
    row = lax.broadcasted_iota(jnp.int32, (QUART, 128), 0)
    pos = pos_ref[0]
    ky = 2 * (64 * (pos % 4) + (lane & 63)) + pos // 4
    ky = jnp.where(ky < HALF, ky, ky - N).astype(F32) * UNIT
    kx = (2 * row + lane // 64).astype(F32) * UNIT
    ky2 = ky * ky
    radial = kx * kx + ky2
    edge = (HALF * UNIT) ** 2 + ky2[:8]
    for f in range(2):
        for r in range(NREF):
            ratio = omega_ref[f] / speed_ref[r]
            square = ratio * ratio
            c, s = phase_of(square - radial)
            cos_ref[f, r] = c
            sin_ref[f, r] = s
            c, s = phase_of(square - edge)
            nyq_ref[f, r, 0] = c
            nyq_ref[f, r, 1] = s


def dest_of(pos, slot):
    chips, core = SLOTS[slot]
    return ((pos // 2 + chips) % 4) * 2 + (pos % 2 + core) % 2


def source_of(pos, slot):
    chips, core = SLOTS[slot]
    return ((pos // 2 + 4 - chips) % 4) * 2 + (pos % 2 + core) % 2


def shift_x(f, pos_ref, lower_ref, came_ref, cos_ref, sin_ref, nyq_ref, ae_ref, ao_ref, be_ref, bo_ref, *refs):
    outs, (spec, swapped, back) = refs[:8], refs[8:]
    near = came_ref[0:4, f].reshape(HALF, 128)
    far = came_ref[4:8, f].reshape(HALF, 128)
    for kind, (mixed, ref) in enumerate(((near + far, ae_ref), (near - far, ao_ref))):
        found = dot3(both(ref), split(mixed))
        spec[kind] = found
        swapped[kind] = pltpu.roll(found, 64, 1)
    first = low_lanes((QUART, 128))
    first8 = low_lanes((8, 128))
    top = lax.broadcasted_iota(jnp.int32, (8, 128), 0) == 0
    inverse = (cat_left(both(be_ref)), cat_left(both(bo_ref)))
    for pair in range(NREF // 2):
        moved = [[], []]
        for r in (2 * pair, 2 * pair + 1):
            c = cos_ref[f, r]
            s = sin_ref[f, r]
            cr = pltpu.roll(c, 64, 1)
            sr = pltpu.roll(s, 64, 1)
            parts = (
                (jnp.where(first, c, cr), jnp.where(first, -s, sr)),
                (jnp.where(first, cr, c), jnp.where(first, -sr, s)),
            )
            nc = nyq_ref[f, r, 0]
            ns = nyq_ref[f, r, 1]
            ns = jnp.where(first8, -ns, ns)
            for kind in range(2):
                blocks = []
                for block in range(2):
                    cc, ss = parts[kind]
                    if kind == 0 and block == 1:
                        cc = jnp.concatenate([jnp.where(top, nc, cc[:8]), cc[8:]], axis=0)
                        ss = jnp.concatenate([jnp.where(top, ns, ss[:8]), ss[8:]], axis=0)
                    rows = pl.ds(QUART * block, QUART)
                    blocks.append(spec[kind, rows, :] * cc + swapped[kind, rows, :] * ss)
                moved[kind].append(split(jnp.concatenate(blocks, axis=0)))
        got = []
        for kind in range(2):
            high = jnp.concatenate([m[0] for m in moved[kind]], axis=1)
            low = jnp.concatenate([m[1] for m in moved[kind]], axis=1)
            got.append(jnp.dot(inverse[kind], cat_right((high, low)), preferred_element_type=F32))
        near, far = got[0] + got[1], got[0] - got[1]
        for i in range(2):
            back[2 * pair + i, 0:HALF] = near[:, 128 * i : 128 * i + 128]
            back[2 * pair + i, HALF:N] = far[:, 128 * i : 128 * i + 128]
    pos = pos_ref[0]
    for slot in range(8):
        p = dest_of(pos, slot)
        base = base_of(lower_ref, p)
        for j in range(NEED):
            outs[slot][j] = back[base + j, pl.ds(pl.multiple_of(64 * p, 64), 64), :]


def base_of(lower_ref, p):
    base = lower_ref[p, 0]
    for q in range(1, 8):
        base = jnp.minimum(base, lower_ref[p, q])
    return jnp.minimum(base, NREF - NEED)


def inverse_y(f, pos_ref, lower_ref, weight_ref, source_ref, even_ref, odd_ref, *refs):
    came = refs[:8]
    pieces = refs[-1]
    pos = pos_ref[0]
    for slot in range(8):
        pieces[source_of(pos, slot)] = came[slot][...]
    first = low_lanes((64, 128))
    halves = []
    for kind, ref in enumerate((even_ref, odd_ref)):
        rows = []
        for j in range(NEED):
            re, im = [], []
            for m in range(2):
                a = pieces[4 * kind + 2 * m, j]
                b = pieces[4 * kind + 2 * m + 1, j]
                re.append(jnp.where(first, a, pltpu.roll(b, 64, 1)))
                im.append(jnp.where(first, pltpu.roll(a, 64, 1), b))
            rows += [jnp.concatenate(re, axis=1), jnp.concatenate(im, axis=1)]
        halves.append(dot3(split(jnp.concatenate(rows, axis=0)), both(ref)))
    base = base_of(lower_ref, pos)
    lane = low_lanes((1, 128))
    coef = []
    for j in range(NEED):
        tiles = []
        for q in range(8):
            lower, weight = lower_ref[pos, q] - base, weight_ref[pos, q]
            tiles.append(jnp.where(lower == j, weight, 0.0) + jnp.where(lower + 1 == j, 1.0 - weight, 0.0))
        coef.append([jnp.where(lane, tiles[2 * t], tiles[2 * t + 1]) for t in range(4)])
    field = [[None] * 4, [None] * 4]
    for j in range(NEED):
        for c in range(2):
            rows = slice(128 * j + 64 * c, 128 * j + 64 * c + 64)
            for t in range(4):
                lanes = slice(128 * (t % 2), 128 * (t % 2) + 128)
                u, v = halves[0][rows, lanes], halves[1][rows, lanes]
                term = (u + v if t < 2 else u - v) * coef[j][t]
                field[c][t] = term if j == 0 else field[c][t] + term
    image = []
    for t in range(4):
        lanes = slice(128 * t, 128 * t + 128)
        image.append(field[0][t] * source_ref[f, :, 0, lanes] + field[1][t] * source_ref[f, :, 1, lanes])
    if f == 0:
        out_ref, part_ref = refs[8:10]
        for t in range(4):
            lanes = slice(128 * t, 128 * t + 128)
            part_ref[:, lanes] = image[t]
            for c in range(2):
                out_ref[c, :, lanes] = field[c][t]
        return
    other_ref, part_ref, out_ref, image_ref = refs[8:12]
    group = lax.broadcasted_iota(jnp.int32, (8, 128), 1) // 16
    for t in range(4):
        lanes = slice(128 * t, 128 * t + 128)
        total = (image[t] + part_ref[:, lanes]) * (1.0 / 8.0)
        cells = [total[8 * b : 8 * b + 8] for b in range(8)]
        for bit in (1, 2, 4):
            low = (group & bit) == 0
            new = [None] * 8
            for b in range(8):
                if b & bit:
                    continue
                x, y = cells[b], cells[b | bit]
                new[b] = jnp.where(low, x, pltpu.roll(y, 16 * bit, 1))
                new[b | bit] = jnp.where(low, pltpu.roll(x, 128 - 16 * bit, 1), y)
            cells = new
        for g in range(8):
            image_ref[8 * t + g] = cells[g]
        for c in range(2):
            out_ref[0, :, c, lanes] = other_ref[c, :, lanes]
            out_ref[1, :, c, lanes] = field[c][t]


def sum_image(came_ref, out_ref):
    total = jnp.sum(came_ref[...], axis=0)
    for b in range(8):
        out_ref[0, 8 * b : 8 * b + 8, :] = total[:, 16 * b : 16 * b + 16]


VM = pl.BlockSpec(memory_space=pltpu.VMEM)
SM = pl.BlockSpec(memory_space=pltpu.SMEM)


def call(body, out, specs, scratch=(), f=None):
    many = isinstance(out, (tuple, list))
    return pl.pallas_call(
        body if f is None else functools.partial(body, f),
        out_shape=out,
        in_specs=specs,
        out_specs=tuple(VM for _ in out) if many else VM,
        scratch_shapes=list(scratch),
        compiler_params=pltpu.CompilerParams(vmem_limit_bytes=16 * 2**20),
        interpret=INTERPRET,
    )


def shape(*dims):
    return jax.ShapeDtypeStruct(dims, F32)


def ring(slot):
    chips, core = SLOTS[slot]
    return [(2 * x + c, 2 * ((x + chips) % 4) + (c + core) % 2) for x in range(4) for c in range(2)]


def whole(wave_field, source_field, omegas, velocities, lower_ref, blend_weight):
    pos = lax.axis_index("pencil").reshape(1)
    even, odd, odd_t, ae, ao, be, bo = (jnp.asarray(t) for t in tables())
    sent = call(forward_y, shape(8, 2, 64, 128), [VM] * 3)(wave_field, even, odd)
    came = lax.all_to_all(sent.reshape(8, 128, 128), "pencil", 0, 0, tiled=True).reshape(8, 2, 64, 128)
    phase = call(
        phases, (shape(2, NREF, QUART, 128), shape(2, NREF, QUART, 128), shape(2, NREF, 2, 8, 128)), [SM] * 3
    )(pos, omegas, velocities[0])
    pieces = []
    for f in range(2):
        sent = call(
            shift_x,
            [shape(NEED, 64, 128)] * 8,
            [SM] * 2 + [VM] * 8,
            [pltpu.VMEM((2, HALF, 128), F32)] * 2 + [pltpu.VMEM((NREF, N, 128), F32)],
            f,
        )(pos, lower_ref[0], came, *phase, ae, ao, be, bo)
        got = []
        for slot in range(7):
            got.append(lax.ppermute(sent[slot], "pencil", ring(slot)))
        pieces.append(got + [sent[7]])
    scratch = [pltpu.VMEM((8, NEED, 64, 128), F32)]
    early = (pos, lower_ref[0], blend_weight[0], source_field[0], even, odd_t)
    specs = [SM] * 3 + [VM] * 11
    part = call(inverse_y, [shape(2, 64, N), shape(64, N)], specs, scratch, 0)(*early, *pieces[0])
    field, image = call(inverse_y, [shape(2, 64, 2, N), shape(32, 8, 128)], specs + [VM] * 2, scratch, 1)(
        *early, *pieces[1], *part
    )
    return finish(field, image)


def finish(field, image):
    came = lax.all_to_all(image, "freq", 0, 0, tiled=True)
    image = call(sum_image, shape(1, 64, 16), [VM])(came)
    return field, image


def solution(mesh):
    placed = (
        P("freq", "pencil", None, None),
        P(None, "freq", "pencil", None, None),
        P("freq"),
        P(),
        P(),
        P(),
    )
    return jax.shard_map(
        whole,
        mesh=mesh,
        in_specs=placed,
        out_specs=(P("freq", "pencil", None, None), P(None, "pencil", "freq")),
        check_vma=False,
    )
```

profile of v0, /device:TPU:2, one launch (start us, length us, event | category | flops | bytes accessed | tf_op | source)
XLA Modules:
  0.0 71.2 jit_solution(1858106774313882875)
XLA Ops:
  0.6 0.0 copy-start
  0.6 0.9 %copy-done = bf16[2,256,256]{2,1,0:T(8,128)(2,1)S(1)} copy-done((bf16[2,256,256]{2,1,0:T(8,128)(2,1)S(1)}, bf16[2,256,256]{2,1,0:T(8,128)(2,1)}, u32[]{:S(2)}) %copy-start) | copy-done | bytes 262168
  1.6 1.0 %copy-done.8 = f32[2,64,2,512]{3,2,1,0:T(2,128)S(1)} copy-done((f32[2,64,2,512]{3,2,1,0:T(2,128)S(1)}, f32[2,64,2,512]{3,2,1,0:T(2,128)}, u32[]{:S(2)}) %copy-start.8) | copy-done | bytes 524312
  2.6 0.9 %copy-done.9 = bf16[2,256,256]{2,1,0:T(8,128)(2,1)S(1)} copy-done((bf16[2,256,256]{2,1,0:T(8,128)(2,1)S(1)}, bf16[2,256,256]{2,1,0:T(8,128)(2,1)}, u32[]{:S(2)}) %copy-start.9) | copy-done | bytes 262168
  3.6 1.3 %shard_map.140 = f32[8,2,64,128]{3,2,1,0:T(8,128)} custom-call(f32[2,64,2,512]{3,2,1,0:T(2,128)S(1)} %copy-done.8, bf16[2,256,256]{2,1,0:T(8,128)(2,1)S(1)} %copy-done, bf16[2,256,256]{2,1,0:T(8,128)(2,1)S(1)} %copy-done.9), custom_call_target="tpu_custom_call" | custom-call | tf_op jit(solution)/shard_map/pallas_call | solution.py:296
  4.9 5.8 %all-to-all-start = ((f32[8,128,128]{2,1,0:T(8,128)}), f32[8,128,128]{2,1,0:T(8,128)S(1)}, u32[]{:S(2)}, u32[]{:S(2)}) async-start(f32[8,128,128]{2,1,0:T(8,128)} %bitcast.4), calls=%async_computation | async-start | bytes 1048576 | tf_op jit(solution)/shard_map/all_to_all | solution.py:297
  10.7 0.7 copy-done.12
  11.4 0.0 copy-done.13
  11.4 2.0 %shard_map.141 = (f32[2,6,128,128]{3,2,1,0:T(8,128)S(1)}, f32[2,6,128,128]{3,2,1,0:T(8,128)S(1)}, f32[2,6,2,8,128]{4,3,2,1,0:T(8,128)S(1)}) custom-call(s32[1]{0:T(128)} %bitcast.pos_ref, f32[2]{0:T(128)S(1)} %copy-done.12, f32[6]{0:T(128)S(1)} %bitcast.17), custom_call_target="tpu_custom_call" | custom-call | tf_op jit(solution)/shard_map/pallas_call | solution.py:298
  13.4 6.2 %all-to-all-done = f32[8,128,128]{2,1,0:T(8,128)S(1)} async-done(((f32[8,128,128]{2,1,0:T(8,128)}), f32[8,128,128]{2,1,0:T(8,128)S(1)}, u32[]{:S(2)}, u32[]{:S(2)}) %all-to-all-start) | async-done | bytes 524320 | tf_op jit(solution)/shard_map/all_to_all | solution.py:297
  19.6 0.0 copy-done.4
  19.6 0.0 copy-done.6
  19.6 0.7 copy-done.10
  20.3 1.9 %shard_map.143 = (f32[3,64,128]{2,1,0:T(8,128)S(1)}, f32[3,64,128]{2,1,0:T(8,128)S(1)}, f32[3,64,128]{2,1,0:T(8,128)S(1)}, f32[3,64,128]{2,1,0:T(8,128)S(1)}, f3...) custom-call(s32[1]{0:T(128)} %bitcast.pos_ref, ...), custom_call_target="tpu_custom_call" | custom-call | tf_op jit(solution)/shard_map/pallas_call | solution.py:303
  22.2 0.1 collective-permute-start.10
  22.3 1.5 %collective-permute-start.11 = (f32[3,64,128]{2,1,0:T(8,128)S(1)}, f32[3,64,128]{2,1,0:T(8,128)S(1)}, u32[]{:S(2)}, u32[]{:S(2)}) collective-permute-start(f32[3,64,128]{2,1,0:T(8,128)S(1)} %get-tuple-element.40), channel_id=1, source_target_pairs={{0,6},{1,7},{2,0},{3,1},{4,2},{5,3},{6,4},{7,5},{8,14},{9,15},{10,... | collective-permute-start | bytes 294920 | tf_op jit(solution)/shard_map/ppermute | solution.py:312
  23.8 2.6 %collective-permute-start.12 = (f32[3,64,128]{2,1,0:T(8,128)S(1)}, f32[3,64,128]{2,1,0:T(8,128)S(1)}, u32[]{:S(2)}, u32[]{:S(2)}) collective-permute-start(f32[3,64,128]{2,1,0:T(8,128)S(1)} %get-tuple-element.41), channel_id=1, source_target_pairs={{0,7},{1,6},{2,1},{3,0},{4,3},{5,2},{6,5},{7,4},{8,15},{9,14},{10,... | collective-permute-start | bytes 294920 | tf_op jit(solution)/shard_map/ppermute | solution.py:312
  26.4 0.0 collective-permute-start.13
  26.4 1.9 %shard_map.142 = (f32[3,64,128]{2,1,0:T(8,128)S(1)}, f32[3,64,128]{2,1,0:T(8,128)S(1)}, f32[3,64,128]{2,1,0:T(8,128)S(1)}, f32[3,64,128]{2,1,0:T(8,128)S(1)}, f3...) custom-call(s32[1]{0:T(128)} %bitcast.pos_ref, ...), custom_call_target="tpu_custom_call" | custom-call | tf_op jit(solution)/shard_map/pallas_call | solution.py:303
  28.3 0.1 collective-permute-start.7
  28.4 0.0 collective-permute-done.10.refs_3_
  28.5 3.3 %collective-permute-start.8 = (f32[3,64,128]{2,1,0:T(8,128)S(1)}, f32[3,64,128]{2,1,0:T(8,128)S(1)}, u32[]{:S(2)}, u32[]{:S(2)}) collective-permute-start(f32[3,64,128]{2,1,0:T(8,128)S(1)} %get-tuple-element.37), channel_id=1, source_target_pairs={{0,5},{1,4},{2,7},{3,6},{4,1},{5,0},{6,3},{7,2},{8,13},{9,12},{10,... | collective-permute-start | bytes 294920 | tf_op jit(solution)/shard_map/ppermute | solution.py:312
  31.8 0.0 collective-permute-done.11.refs_4_
  31.8 0.0 collective-permute-start.9
  31.8 0.0 collective-permute-done.12.refs_5_
  31.8 4.2 %collective-permute-start = (f32[3,64,128]{2,1,0:T(8,128)S(1)}, f32[3,64,128]{2,1,0:T(8,128)S(1)}, u32[]{:S(2)}, u32[]{:S(2)}) collective-permute-start(f32[3,64,128]{2,1,0:T(8,128)S(1)} %get-tuple-element.28), channel_id=1, source_target_pairs={{0,4},{1,5},{2,6},{3,7},{4,0},{5,1},{6,2},{7,3},{8,12},{9,13},{10,... | collective-permute-start | bytes 294920 | tf_op jit(solution)/shard_map/ppermute | solution.py:312
  36.0 0.0 collective-permute-done.13.refs_6_
  36.0 0.0 collective-permute-start.1
  36.0 0.0 collective-permute-done.7.refs_0_
  36.0 0.1 collective-permute-start.2
  36.1 0.6 collective-permute-done.8.refs_1_
  36.7 2.8 %collective-permute-start.3 = (f32[3,64,128]{2,1,0:T(8,128)S(1)}, f32[3,64,128]{2,1,0:T(8,128)S(1)}, u32[]{:S(2)}, u32[]{:S(2)}) collective-permute-start(f32[3,64,128]{2,1,0:T(8,128)S(1)} %get-tuple-element.31), channel_id=1, source_target_pairs={{0,3},{1,2},{2,5},{3,4},{4,7},{5,6},{6,1},{7,0},{8,11},{9,10},{10,... | collective-permute-start | bytes 294920 | tf_op jit(solution)/shard_map/ppermute | solution.py:312
  39.6 0.0 collective-permute-done.9.refs_2_
  39.6 0.7 collective-permute-start.4
  40.3 0.0 collective-permute-done.refs_0_
  40.3 0.6 collective-permute-start.5
  40.8 1.8 %collective-permute-done.1.refs_1_ = f32[3,64,128]{2,1,0:T(8,128)S(1)} collective-permute-done((f32[3,64,128]{2,1,0:T(8,128)S(1)}, f32[3,64,128]{2,1,0:T(8,128)S(1)}, u32[]{:S(2)}, u32[]{:S(2)}) %collective-permute-start.1) | collective-permute-done | bytes 98336 | tf_op jit(solution)/shard_map/ppermute | solution.py:312
  42.7 0.1 collective-permute-start.6
  42.8 1.6 %shard_map.144 = (f32[2,64,512]{2,1,0:T(8,128)S(1)}, f32[64,512]{1,0:T(8,128)S(1)}) custom-call(s32[1]{0:T(128)} %bitcast.pos_ref, s32[8,8]{1,0:T(8,128)S(1)} %bitcast.13, f32[8,8]{1,0:T(8,128)S(1)} %bitcast.15, f32[2,64,2,512]{3,2,1,0:T(2,128)S(1)} %bitcast.9, bf16[2,256,256]{2,1,0:T(8,128)(2,1)S(1)} %copy-done.1, bf16[2,256,256]{2,1,0:T(8,128)(2,1)S(1)} %copy-done.3, ...), custom_call_target="tpu_custom_call" | custom-call | tf_op jit(solution)/shard_map/pallas_call | solution.py:317
  44.3 0.0 collective-permute-done.2.refs_2_
  44.3 1.6 %collective-permute-done.3.refs_3_ = f32[3,64,128]{2,1,0:T(8,128)S(1)} collective-permute-done((f32[3,64,128]{2,1,0:T(8,128)S(1)}, f32[3,64,128]{2,1,0:T(8,128)S(1)}, u32[]{:S(2)}, u32[]{:S(2)}) %collective-permute-start.3) | collective-permute-done | bytes 98336 | tf_op jit(solution)/shard_map/ppermute | solution.py:312
  45.9 0.0 collective-permute-done.4.refs_4_
  45.9 0.4 collective-permute-done.5.refs_5_
  46.3 0.0 collective-permute-done.6.refs_6_
  46.3 2.8 %shard_map.145 = (f32[2,64,2,512]{3,2,1,0:T(2,128)}, f32[32,8,128]{2,1,0:T(8,128)S(1)}) custom-call(s32[1]{0:T(128)} %bitcast.pos_ref, s32[8,8]{1,0:T(8,128)S(1)} %bitcast.14, f32[8,8]{1,0:T(8,128)S(1)} %bitcast.16, f32[2,64,2,512]{3,2,1,0:T(2,128)S(1)} %bitcast.10, bf16[2,256,256]{2,1,0:T(8,128)(2,1)S(1)} %copy-done.1, bf16[2,256,256]{2,1,0:T(8,128)(2,1)S(1)} %copy-done.3, ...), custom_call_target="tpu_custom_call" | custom-call | tf_op jit(solution)/shard_map/pallas_call | solution.py:318
  49.1 21.3 %all_to_all.10.came_ref = f32[32,8,128]{2,1,0:T(8,128)S(1)} all-to-all(f32[32,8,128]{2,1,0:T(8,128)S(1)} %get-tuple-element.47), channel_id=1, replica_groups=mesh['freq'=32,'pencil'=8] {'freq'}, dimensions={0} | all-to-all | bytes 262144 | tf_op jit(solution)/shard_map/all_to_all | solution.py:325
  70.4 0.1 shard_map.146
  70.5 0.7 copy.15
  (19 shorter events, 0.0 us)
Async XLA Ops:
  0.6 1.0 %copy-start = (bf16[2,256,256]{2,1,0:T(8,128)(2,1)S(1)}, bf16[2,256,256]{2,1,0:T(8,128)(2,1)}, u32[]{:S(2)}) copy-start(bf16[2,256,256]{2,1,0:T(8,128)(2,1)} %constant.18.clone.even_ref) | copy-start | bytes 786436
  1.6 1.0 %copy-start.8 = (f32[2,64,2,512]{3,2,1,0:T(2,128)S(1)}, f32[2,64,2,512]{3,2,1,0:T(2,128)}, u32[]{:S(2)}) copy-start(f32[2,64,2,512]{3,2,1,0:T(2,128)} %wave_ref.1) | copy-start | bytes 1572868
  2.6 0.9 %copy-start.9 = (bf16[2,256,256]{2,1,0:T(8,128)(2,1)S(1)}, bf16[2,256,256]{2,1,0:T(8,128)(2,1)}, u32[]{:S(2)}) copy-start(bf16[2,256,256]{2,1,0:T(8,128)(2,1)} %constant.19.clone.odd_ref) | copy-start | bytes 786436
  4.9 14.7 %copy-start.4 = (bf16[2,256,256]{2,1,0:T(8,128)(2,1)S(1)}, bf16[2,256,256]{2,1,0:T(8,128)(2,1)}, u32[]{:S(2)}) copy-start(bf16[2,256,256]{2,1,0:T(8,128)(2,1)} %constant.21.clone.ae_ref) | copy-start | bytes 786436
  4.9 14.7 %copy-start.5 = (bf16[2,256,256]{2,1,0:T(8,128)(2,1)S(1)}, bf16[2,256,256]{2,1,0:T(8,128)(2,1)}, u32[]{:S(2)}) copy-start(bf16[2,256,256]{2,1,0:T(8,128)(2,1)} %constant.22.clone.ao_ref) | copy-start | bytes 786436
  4.9 14.7 %copy-start.6 = (bf16[2,256,256]{2,1,0:T(8,128)(2,1)S(1)}, bf16[2,256,256]{2,1,0:T(8,128)(2,1)}, u32[]{:S(2)}) copy-start(bf16[2,256,256]{2,1,0:T(8,128)(2,1)} %constant.23.clone.be_ref) | copy-start | bytes 786436
  4.9 14.7 %copy-start.7 = (bf16[2,256,256]{2,1,0:T(8,128)(2,1)S(1)}, bf16[2,256,256]{2,1,0:T(8,128)(2,1)}, u32[]{:S(2)}) copy-start(bf16[2,256,256]{2,1,0:T(8,128)(2,1)} %constant.24.clone.bo_ref) | copy-start | bytes 786436
  4.9 14.7 %all-to-all-start = ((f32[8,128,128]{2,1,0:T(8,128)}), f32[8,128,128]{2,1,0:T(8,128)S(1)}, u32[]{:S(2)}, u32[]{:S(2)}) async-start(f32[8,128,128]{2,1,0:T(8,128)} %bitcast.4), calls=%async_computation | async-start | bytes 1048576 | tf_op jit(solution)/shard_map/all_to_all | solution.py:297
  10.7 0.7 copy-start.12
  10.7 0.7 copy-start.13
  19.6 0.7 copy-start.10
  22.2 6.2 %collective-permute-start.10 = (f32[3,64,128]{2,1,0:T(8,128)S(1)}, f32[3,64,128]{2,1,0:T(8,128)S(1)}, u32[]{:S(2)}, u32[]{:S(2)}) collective-permute-start(f32[3,64,128]{2,1,0:T(8,128)S(1)} %get-tuple-element.39), channel_id=1, source_target_pairs={{0,3},{1,2},{2,5},{3,4},{4,7},{5,6},{6,1},{7,0},{8,11},{9,10},{10,... | collective-permute-start | bytes 294920 | tf_op jit(solution)/shard_map/ppermute | solution.py:312
  22.3 9.5 %collective-permute-start.11 = (f32[3,64,128]{2,1,0:T(8,128)S(1)}, f32[3,64,128]{2,1,0:T(8,128)S(1)}, u32[]{:S(2)}, u32[]{:S(2)}) collective-permute-start(f32[3,64,128]{2,1,0:T(8,128)S(1)} %get-tuple-element.40), channel_id=1, source_target_pairs={{0,6},{1,7},{2,0},{3,1},{4,2},{5,3},{6,4},{7,5},{8,14},{9,15},{10,... | collective-permute-start | bytes 294920 | tf_op jit(solution)/shard_map/ppermute | solution.py:312
  23.8 8.0 %collective-permute-start.12 = (f32[3,64,128]{2,1,0:T(8,128)S(1)}, f32[3,64,128]{2,1,0:T(8,128)S(1)}, u32[]{:S(2)}, u32[]{:S(2)}) collective-permute-start(f32[3,64,128]{2,1,0:T(8,128)S(1)} %get-tuple-element.41), channel_id=1, source_target_pairs={{0,7},{1,6},{2,1},{3,0},{4,3},{5,2},{6,5},{7,4},{8,15},{9,14},{10,... | collective-permute-start | bytes 294920 | tf_op jit(solution)/shard_map/ppermute | solution.py:312
  26.4 16.3 %copy-start.1 = (bf16[2,256,256]{2,1,0:T(8,128)(2,1)S(1)}, bf16[2,256,256]{2,1,0:T(8,128)(2,1)}, u32[]{:S(2)}) copy-start(bf16[2,256,256]{2,1,0:T(8,128)(2,1)} %constant.18.clone.even_ref) | copy-start | bytes 786436
  26.4 16.3 %copy-start.2 = (f32[1,2,64,2,512]{4,3,2,1,0:T(2,128)S(1)}, f32[1,2,64,2,512]{4,3,2,1,0:T(2,128)}, u32[]{:S(2)}) copy-start(f32[1,2,64,2,512]{4,3,2,1,0:T(2,128)} %param.14) | copy-start | bytes 1572868
  26.4 16.3 %copy-start.3 = (bf16[2,256,256]{2,1,0:T(8,128)(2,1)S(1)}, bf16[2,256,256]{2,1,0:T(8,128)(2,1)}, u32[]{:S(2)}) copy-start(bf16[2,256,256]{2,1,0:T(8,128)(2,1)} %constant.20.clone.odd_ref) | copy-start | bytes 786436
  26.4 9.6 %collective-permute-start.13 = (f32[3,64,128]{2,1,0:T(8,128)S(1)}, f32[3,64,128]{2,1,0:T(8,128)S(1)}, u32[]{:S(2)}, u32[]{:S(2)}) collective-permute-start(f32[3,64,128]{2,1,0:T(8,128)S(1)} %get-tuple-element.42), channel_id=1, source_target_pairs={{0,1},{1,0},{2,3},{3,2},{4,5},{5,4},{6,7},{7,6},{8,9},{9,8},{10,11... | collective-permute-start | bytes 294920 | tf_op jit(solution)/shard_map/ppermute | solution.py:312
  28.3 7.7 %collective-permute-start.7 = (f32[3,64,128]{2,1,0:T(8,128)S(1)}, f32[3,64,128]{2,1,0:T(8,128)S(1)}, u32[]{:S(2)}, u32[]{:S(2)}) collective-permute-start(f32[3,64,128]{2,1,0:T(8,128)S(1)} %get-tuple-element.36), channel_id=1, source_target_pairs={{0,4},{1,5},{2,6},{3,7},{4,0},{5,1},{6,2},{7,3},{8,12},{9,13},{10,... | collective-permute-start | bytes 294920 | tf_op jit(solution)/shard_map/ppermute | solution.py:312
  28.5 8.3 %collective-permute-start.8 = (f32[3,64,128]{2,1,0:T(8,128)S(1)}, f32[3,64,128]{2,1,0:T(8,128)S(1)}, u32[]{:S(2)}, u32[]{:S(2)}) collective-permute-start(f32[3,64,128]{2,1,0:T(8,128)S(1)} %get-tuple-element.37), channel_id=1, source_target_pairs={{0,5},{1,4},{2,7},{3,6},{4,1},{5,0},{6,3},{7,2},{8,13},{9,12},{10,... | collective-permute-start | bytes 294920 | tf_op jit(solution)/shard_map/ppermute | solution.py:312
  31.8 7.8 %collective-permute-start.9 = (f32[3,64,128]{2,1,0:T(8,128)S(1)}, f32[3,64,128]{2,1,0:T(8,128)S(1)}, u32[]{:S(2)}, u32[]{:S(2)}) collective-permute-start(f32[3,64,128]{2,1,0:T(8,128)S(1)} %get-tuple-element.38), channel_id=1, source_target_pairs={{0,2},{1,3},{2,4},{3,5},{4,6},{5,7},{6,0},{7,1},{8,10},{9,11},{10,... | collective-permute-start | bytes 294920 | tf_op jit(solution)/shard_map/ppermute | solution.py:312
  31.8 8.5 %collective-permute-start = (f32[3,64,128]{2,1,0:T(8,128)S(1)}, f32[3,64,128]{2,1,0:T(8,128)S(1)}, u32[]{:S(2)}, u32[]{:S(2)}) collective-permute-start(f32[3,64,128]{2,1,0:T(8,128)S(1)} %get-tuple-element.28), channel_id=1, source_target_pairs={{0,4},{1,5},{2,6},{3,7},{4,0},{5,1},{6,2},{7,3},{8,12},{9,13},{10,... | collective-permute-start | bytes 294920 | tf_op jit(solution)/shard_map/ppermute | solution.py:312
  36.0 6.6 %collective-permute-start.1 = (f32[3,64,128]{2,1,0:T(8,128)S(1)}, f32[3,64,128]{2,1,0:T(8,128)S(1)}, u32[]{:S(2)}, u32[]{:S(2)}) collective-permute-start(f32[3,64,128]{2,1,0:T(8,128)S(1)} %get-tuple-element.29), channel_id=1, source_target_pairs={{0,5},{1,4},{2,7},{3,6},{4,1},{5,0},{6,3},{7,2},{8,13},{9,12},{10,... | collective-permute-start | bytes 294920 | tf_op jit(solution)/shard_map/ppermute | solution.py:312
  36.0 8.3 %collective-permute-start.2 = (f32[3,64,128]{2,1,0:T(8,128)S(1)}, f32[3,64,128]{2,1,0:T(8,128)S(1)}, u32[]{:S(2)}, u32[]{:S(2)}) collective-permute-start(f32[3,64,128]{2,1,0:T(8,128)S(1)} %get-tuple-element.30), channel_id=1, source_target_pairs={{0,2},{1,3},{2,4},{3,5},{4,6},{5,7},{6,0},{7,1},{8,10},{9,11},{10,... | collective-permute-start | bytes 294920 | tf_op jit(solution)/shard_map/ppermute | solution.py:312
  36.7 9.2 %collective-permute-start.3 = (f32[3,64,128]{2,1,0:T(8,128)S(1)}, f32[3,64,128]{2,1,0:T(8,128)S(1)}, u32[]{:S(2)}, u32[]{:S(2)}) collective-permute-start(f32[3,64,128]{2,1,0:T(8,128)S(1)} %get-tuple-element.31), channel_id=1, source_target_pairs={{0,3},{1,2},{2,5},{3,4},{4,7},{5,6},{6,1},{7,0},{8,11},{9,10},{10,... | collective-permute-start | bytes 294920 | tf_op jit(solution)/shard_map/ppermute | solution.py:312
  39.6 6.3 %collective-permute-start.4 = (f32[3,64,128]{2,1,0:T(8,128)S(1)}, f32[3,64,128]{2,1,0:T(8,128)S(1)}, u32[]{:S(2)}, u32[]{:S(2)}) collective-permute-start(f32[3,64,128]{2,1,0:T(8,128)S(1)} %get-tuple-element.32), channel_id=1, source_target_pairs={{0,6},{1,7},{2,0},{3,1},{4,2},{5,3},{6,4},{7,5},{8,14},{9,15},{10,... | collective-permute-start | bytes 294920 | tf_op jit(solution)/shard_map/ppermute | solution.py:312
  40.3 2.5 %copy-start.11 = (f32[1,8,8]{2,1,0:T(8,128)S(1)}, f32[1,8,8]{2,1,0:T(8,128)}, u32[]{:S(2)}) copy-start(f32[1,8,8]{2,1,0:T(8,128)} %param.18) | copy-start | bytes 772
  40.3 6.0 %collective-permute-start.5 = (f32[3,64,128]{2,1,0:T(8,128)S(1)}, f32[3,64,128]{2,1,0:T(8,128)S(1)}, u32[]{:S(2)}, u32[]{:S(2)}) collective-permute-start(f32[3,64,128]{2,1,0:T(8,128)S(1)} %get-tuple-element.33), channel_id=1, source_target_pairs={{0,7},{1,6},{2,1},{3,0},{4,3},{5,2},{6,5},{7,4},{8,15},{9,14},{10,... | collective-permute-start | bytes 294920 | tf_op jit(solution)/shard_map/ppermute | solution.py:312
  42.7 3.7 %collective-permute-start.6 = (f32[3,64,128]{2,1,0:T(8,128)S(1)}, f32[3,64,128]{2,1,0:T(8,128)S(1)}, u32[]{:S(2)}, u32[]{:S(2)}) collective-permute-start(f32[3,64,128]{2,1,0:T(8,128)S(1)} %get-tuple-element.34), channel_id=1, source_target_pairs={{0,1},{1,0},{2,3},{3,2},{4,5},{5,4},{6,7},{7,6},{8,9},{9,8},{10,11... | collective-permute-start | bytes 294920 | tf_op jit(solution)/shard_map/ppermute | solution.py:312
where the time goes:
time: 71.9 us; the launch traced here: 71.2 us
  starting transfers between devices  21.9 us (30%)
  blocking collectives  21.3 us (30%)
  Pallas kernels  11.6 us (16%)
  waiting for transfers between devices  10.7 us (15%)
  local copies, waits for them, and re-layouts  4.98 us (7%)
  between operations  0.76 us (1%)
    all_to_all x1, blocking collectives, finish(): came = lax.all_to_all(image, 'freq', 0, 0, tiled=True)  21.3 us
    ppermute x14, starting transfers between devices, whole(): got.append(lax.ppermute(sent[slot], 'pencil', ring(slot)))  16.1 us
    all_to_all x1, waiting for transfers between devices, whole(): lax.all_to_all(sent.reshape(8, 128, 128), 'pencil', 0, 0, tiled=True)  6.24 us
    all_to_all x1, starting transfers between devices, whole(): lax.all_to_all(sent.reshape(8, 128, 128), 'pencil', 0, 0, tiled=True)  5.79 us
    unnamed x29, local copies, waits for them, and re-layouts  4.98 us
    ppermute x14, waiting for transfers between devices, whole(): got.append(lax.ppermute(sent[slot], 'pencil', ring(slot)))  4.46 us
    pallas_call x2, Pallas kernels, whole(): call(shift_x, [shape(NEED, 64, 128)] * 8, [SM] * 2 + [VM] * 8, [pltpu.VME...  3.81 us
    pallas_call x1, Pallas kernels, whole(): call(inverse_y, [shape(2, 64, 2, N), shape(32, 8, 128)], specs + [VM] * 2...  2.81 us
  transfers between devices with their start and end apart: 15, of which 5 were waited for; matrix products, arithmetic and copies ran while one was open for 0% of the time, Pallas kernels for 8%

commit v1 on v0

--- a/solution.py
+++ b/solution.py
@@ -65,7 +65,14 @@
     return lax.broadcasted_iota(jnp.int32, shape, len(shape) - 1) < 64
 
 
-def forward_y(wave_ref, even_ref, odd_ref, out_ref):
+def forward_y(pos_ref, wave_hbm, even_hbm, odd_hbm, *refs):
+    outs, (wave_ref, even_ref, odd_ref, sem, ready) = refs[:8], refs[8:]
+    pairs = ((wave_hbm, wave_ref), (even_hbm, even_ref), (odd_hbm, odd_ref))
+    copies = [pltpu.make_async_copy(src, dst, sem.at[i]) for i, (src, dst) in enumerate(pairs)]
+    for copy in copies:
+        copy.start()
+    for copy in copies:
+        copy.wait()
     rows = jnp.concatenate([wave_ref[f, :, c, :] for f in range(2) for c in range(2)], axis=0)
     near, far = rows[:, :HALF], rows[:, HALF:]
     first = low_lanes((64, 128))
@@ -76,8 +83,10 @@
                 lanes = slice(128 * m, 128 * m + 128)
                 re = spectrum[128 * f : 128 * f + 64, lanes]
                 im = spectrum[128 * f + 64 : 128 * f + 128, lanes]
-                out_ref[4 * kind + 2 * m, f] = jnp.where(first, re, pltpu.roll(im, 64, 1))
-                out_ref[4 * kind + 2 * m + 1, f] = jnp.where(first, pltpu.roll(re, 64, 1), im)
+                ready[4 * kind + 2 * m, f] = jnp.where(first, re, pltpu.roll(im, 64, 1))
+                ready[4 * kind + 2 * m + 1, f] = jnp.where(first, pltpu.roll(re, 64, 1), im)
+    for slot in range(8):
+        outs[slot][...] = ready[dest_of(pos_ref[0], slot)]
 
 
 def phase_of(q):
@@ -126,10 +135,15 @@
     return ((pos // 2 + 4 - chips) % 4) * 2 + (pos % 2 + core) % 2
 
 
-def shift_x(f, pos_ref, lower_ref, came_ref, cos_ref, sin_ref, nyq_ref, ae_ref, ao_ref, be_ref, bo_ref, *refs):
-    outs, (spec, swapped, back) = refs[:8], refs[8:]
-    near = came_ref[0:4, f].reshape(HALF, 128)
-    far = came_ref[4:8, f].reshape(HALF, 128)
+def shift_x(f, pos_ref, lower_hbm, cos_ref, sin_ref, nyq_ref, ae_ref, ao_ref, be_ref, bo_ref, *refs):
+    came, outs, (spec, swapped, back, lower_ref, sem, wave) = refs[:8], refs[8:16], refs[16:]
+    fetch = pltpu.make_async_copy(lower_hbm, lower_ref, sem)
+    fetch.start()
+    pos = pos_ref[0]
+    for slot in range(8):
+        wave[source_of(pos, slot)] = came[slot][f]
+    near = wave[0:4].reshape(HALF, 128)
+    far = wave[4:8].reshape(HALF, 128)
     for kind, (mixed, ref) in enumerate(((near + far, ae_ref), (near - far, ao_ref))):
         found = dot3(both(ref), split(mixed))
         spec[kind] = found
@@ -171,7 +185,7 @@
         for i in range(2):
             back[2 * pair + i, 0:HALF] = near[:, 128 * i : 128 * i + 128]
             back[2 * pair + i, HALF:N] = far[:, 128 * i : 128 * i + 128]
-    pos = pos_ref[0]
+    fetch.wait()
     for slot in range(8):
         p = dest_of(pos, slot)
         base = base_of(lower_ref, p)
@@ -180,15 +194,21 @@
 
 
 def base_of(lower_ref, p):
-    base = lower_ref[p, 0]
+    base = lower_ref[0, p, 0]
     for q in range(1, 8):
-        base = jnp.minimum(base, lower_ref[p, q])
+        base = jnp.minimum(base, lower_ref[0, p, q])
     return jnp.minimum(base, NREF - NEED)
 
 
-def inverse_y(f, pos_ref, lower_ref, weight_ref, source_ref, even_ref, odd_ref, *refs):
+def inverse_y(f, pos_ref, lower_hbm, weight_hbm, source_ref, even_ref, odd_ref, *refs):
     came = refs[:8]
-    pieces = refs[-1]
+    pieces, lower_ref, weight_ref, sem = refs[-4:]
+    fetches = (
+        pltpu.make_async_copy(lower_hbm, lower_ref, sem.at[0]),
+        pltpu.make_async_copy(weight_hbm, weight_ref, sem.at[1]),
+    )
+    for fetch in fetches:
+        fetch.start()
     pos = pos_ref[0]
     for slot in range(8):
         pieces[source_of(pos, slot)] = came[slot][...]
@@ -205,13 +225,15 @@
                 im.append(jnp.where(first, pltpu.roll(a, 64, 1), b))
             rows += [jnp.concatenate(re, axis=1), jnp.concatenate(im, axis=1)]
         halves.append(dot3(split(jnp.concatenate(rows, axis=0)), both(ref)))
+    for fetch in fetches:
+        fetch.wait()
     base = base_of(lower_ref, pos)
     lane = low_lanes((1, 128))
     coef = []
     for j in range(NEED):
         tiles = []
         for q in range(8):
-            lower, weight = lower_ref[pos, q] - base, weight_ref[pos, q]
+            lower, weight = lower_ref[0, pos, q] - base, weight_ref[0, pos, q]
             tiles.append(jnp.where(lower == j, weight, 0.0) + jnp.where(lower + 1 == j, 1.0 - weight, 0.0))
         coef.append([jnp.where(lane, tiles[2 * t], tiles[2 * t + 1]) for t in range(4)])
     field = [[None] * 4, [None] * 4]
@@ -227,15 +249,16 @@
     for t in range(4):
         lanes = slice(128 * t, 128 * t + 128)
         image.append(field[0][t] * source_ref[f, :, 0, lanes] + field[1][t] * source_ref[f, :, 1, lanes])
+    out_ref, image_ref = refs[8:10] if f == 0 else refs[9:11]
+    for t in range(4):
+        lanes = slice(128 * t, 128 * t + 128)
+        for c in range(2):
+            out_ref[c, :, lanes] = field[c][t]
+        if f == 0:
+            image_ref[:, lanes] = image[t]
     if f == 0:
-        out_ref, part_ref = refs[8:10]
-        for t in range(4):
-            lanes = slice(128 * t, 128 * t + 128)
-            part_ref[:, lanes] = image[t]
-            for c in range(2):
-                out_ref[c, :, lanes] = field[c][t]
         return
-    other_ref, part_ref, out_ref, image_ref = refs[8:12]
+    part_ref = refs[8]
     group = lax.broadcasted_iota(jnp.int32, (8, 128), 1) // 16
     for t in range(4):
         lanes = slice(128 * t, 128 * t + 128)
@@ -253,22 +276,26 @@
             cells = new
         for g in range(8):
             image_ref[8 * t + g] = cells[g]
+
+
+def store_field(first_ref, second_ref, out_ref):
+    for f, ref in enumerate((first_ref, second_ref)):
         for c in range(2):
-            out_ref[0, :, c, lanes] = other_ref[c, :, lanes]
-            out_ref[1, :, c, lanes] = field[c][t]
+            out_ref[f, :, c, :] = ref[c]
 
 
 def sum_image(came_ref, out_ref):
-    total = jnp.sum(came_ref[...], axis=0)
-    for b in range(8):
-        out_ref[0, 8 * b : 8 * b + 8, :] = total[:, 16 * b : 16 * b + 16]
+    total = jnp.sum(came_ref[...], axis=0).T
+    out_ref[0] = jnp.concatenate([total[16 * b : 16 * b + 16] for b in range(8)], axis=1)
 
 
 VM = pl.BlockSpec(memory_space=pltpu.VMEM)
 SM = pl.BlockSpec(memory_space=pltpu.SMEM)
-
-
-def call(body, out, specs, scratch=(), f=None):
+HB = pl.BlockSpec(memory_space=pltpu.HBM)
+TILES = (1, 8, 8)
+
+
+def call(body, out, specs, scratch=(), f=None, grant=16):
     many = isinstance(out, (tuple, list))
     return pl.pallas_call(
         body if f is None else functools.partial(body, f),
@@ -276,7 +303,7 @@
         in_specs=specs,
         out_specs=tuple(VM for _ in out) if many else VM,
         scratch_shapes=list(scratch),
-        compiler_params=pltpu.CompilerParams(vmem_limit_bytes=16 * 2**20),
+        compiler_params=pltpu.CompilerParams(vmem_limit_bytes=grant * 2**20),
         interpret=INTERPRET,
     )
 
@@ -290,11 +317,30 @@
     return [(2 * x + c, 2 * ((x + chips) % 4) + (c + core) % 2) for x in range(4) for c in range(2)]
 
 
+def exchange(sent):
+    got = []
+    for slot in range(7):
+        got.append(lax.ppermute(sent[slot], "pencil", ring(slot)))
+    return got + [sent[7]]
+
+
 def whole(wave_field, source_field, omegas, velocities, lower_ref, blend_weight):
     pos = lax.axis_index("pencil").reshape(1)
     even, odd, odd_t, ae, ao, be, bo = (jnp.asarray(t) for t in tables())
-    sent = call(forward_y, shape(8, 2, 64, 128), [VM] * 3)(wave_field, even, odd)
-    came = lax.all_to_all(sent.reshape(8, 128, 128), "pencil", 0, 0, tiled=True).reshape(8, 2, 64, 128)
+    sent = call(
+        forward_y,
+        [shape(2, 64, 128)] * 8,
+        [SM] + [HB] * 3,
+        [
+            pltpu.VMEM(wave_field.shape, F32),
+            pltpu.VMEM(even.shape, BF),
+            pltpu.VMEM(odd.shape, BF),
+            pltpu.SemaphoreType.DMA((3,)),
+            pltpu.VMEM((8, 2, 64, 128), F32),
+        ],
+        grant=60,
+    )(pos, wave_field, even, odd)
+    came = exchange(sent)
     phase = call(
         phases, (shape(2, NREF, QUART, 128), shape(2, NREF, QUART, 128), shape(2, NREF, 2, 8, 128)), [SM] * 3
     )(pos, omegas, velocities[0])
@@ -303,28 +349,33 @@
         sent = call(
             shift_x,
             [shape(NEED, 64, 128)] * 8,
-            [SM] * 2 + [VM] * 8,
-            [pltpu.VMEM((2, HALF, 128), F32)] * 2 + [pltpu.VMEM((NREF, N, 128), F32)],
+            [SM, HB] + [VM] * 15,
+            [pltpu.VMEM((2, HALF, 128), F32)] * 2
+            + [pltpu.VMEM((NREF, N, 128), F32), pltpu.SMEM(TILES, jnp.int32), pltpu.SemaphoreType.DMA]
+            + [pltpu.VMEM((8, 64, 128), F32)],
             f,
-        )(pos, lower_ref[0], came, *phase, ae, ao, be, bo)
-        got = []
-        for slot in range(7):
-            got.append(lax.ppermute(sent[slot], "pencil", ring(slot)))
-        pieces.append(got + [sent[7]])
-    scratch = [pltpu.VMEM((8, NEED, 64, 128), F32)]
-    early = (pos, lower_ref[0], blend_weight[0], source_field[0], even, odd_t)
-    specs = [SM] * 3 + [VM] * 11
-    part = call(inverse_y, [shape(2, 64, N), shape(64, N)], specs, scratch, 0)(*early, *pieces[0])
-    field, image = call(inverse_y, [shape(2, 64, 2, N), shape(32, 8, 128)], specs + [VM] * 2, scratch, 1)(
-        *early, *pieces[1], *part
-    )
-    return finish(field, image)
-
-
-def finish(field, image):
+        )(pos, lower_ref, *phase, ae, ao, be, bo, *came)
+        pieces.append(exchange(sent))
+    scratch = [
+        pltpu.VMEM((8, NEED, 64, 128), F32),
+        pltpu.SMEM(TILES, jnp.int32),
+        pltpu.SMEM(TILES, F32),
+        pltpu.SemaphoreType.DMA((2,)),
+    ]
+    early = (pos, lower_ref, blend_weight, source_field[0], even, odd_t)
+    specs = [SM, HB, HB] + [VM] * 11
+    first, part = call(inverse_y, [shape(2, 64, N), shape(64, N)], specs, scratch, 0)(*early, *pieces[0])
+    second, image = call(inverse_y, [shape(2, 64, N), shape(32, 8, 128)], specs + [VM], scratch, 1)(
+        *early, *pieces[1], part
+    )
+    return finish(first, second, image)
+
+
+def finish(first, second, image):
     came = lax.all_to_all(image, "freq", 0, 0, tiled=True)
-    image = call(sum_image, shape(1, 64, 16), [VM])(came)
-    return field, image
+    field = call(store_field, shape(2, 64, 2, N), [VM] * 2)(first, second)
+    image = call(sum_image, shape(1, 16, 64), [VM])(came)
+    return field, jnp.transpose(image, (0, 2, 1))
 
 
 def solution(mesh):

time: 71.9 us -> 66 us (0.918)
  blocking collectives: 21.3 us -> 0 us
  starting transfers between devices: 21.9 us -> 37.4 us
  local copies, waits for them, and re-layouts: 4.98 us -> 1.3 us
  waiting for transfers between devices: 10.7 us -> 13.5 us
    all_to_all x1 -> x0, blocking collectives: 21.3 us -> none  [finish(): came = lax.all_to_all(image, 'freq', 0, 0, tiled=True)]
    ppermute x14 -> x21, starting transfers between devices: 16.1 us -> 26.5 us  [exchange(): got.append(lax.ppermute(sent[slot], 'pencil', ring(slot)))]
    all_to_all x1, starting transfers between devices: 5.79 us -> 10.9 us  [finish(): came = lax.all_to_all(image, 'freq', 0, 0, tiled=True)]
    unnamed x29 -> x24, local copies, waits for them, and re-layouts: 4.98 us -> 1.3 us
    all_to_all x1, waiting for transfers between devices: 6.24 us -> 9.69 us  [finish(): came = lax.all_to_all(image, 'freq', 0, 0, tiled=True)]
    pallas_call x5 -> x6, Pallas kernels: 8.07 us -> 9.29 us  [the longest x2 2.95 us: whole(): call(shift_x, [shape(NEED, 64, 128)] * 8, [SM, HB] + [VM] * 15, [pltpu.VM...]
    ppermute x14 -> x21, waiting for transfers between devices: 4.46 us -> 3.83 us  [exchange(): got.append(lax.ppermute(sent[slot], 'pencil', ring(slot)))]
  transfers between devices with their start and end apart: 15 -> 22, of which waited for: 5 -> 5; matrix products, arithmetic and copies ran while one was open for 0% -> 0% of each run, Pallas kernels for 8% -> 8%
where the time goes in v1:
time: 66 us; the launch traced here: 65.3 us
  starting transfers between devices  37.4 us (57%)
  waiting for transfers between devices  13.5 us (20%)
  Pallas kernels  12.3 us (19%)
  local copies, waits for them, and re-layouts  1.3 us (2%)
  between operations  0.81 us (1%)
    ppermute x21, starting transfers between devices, exchange(): got.append(lax.ppermute(sent[slot], 'pencil', ring(slot)))  26.5 us
    all_to_all x1, starting transfers between devices, finish(): came = lax.all_to_all(image, 'freq', 0, 0, tiled=True)  10.9 us
    all_to_all x1, waiting for transfers between devices, finish(): came = lax.all_to_all(image, 'freq', 0, 0, tiled=True)  9.69 us
    ppermute x21, waiting for transfers between devices, exchange(): got.append(lax.ppermute(sent[slot], 'pencil', ring(slot)))  3.83 us
    pallas_call x2, Pallas kernels, whole(): call(shift_x, [shape(NEED, 64, 128)] * 8, [SM, HB] + [VM] * 15, [pltpu.VM...  2.95 us
    pallas_call x1, Pallas kernels, whole(): call(forward_y, [shape(2, 64, 128)] * 8, [SM] + [HB] * 3, [pltpu.VMEM(wav...  2.63 us
    pallas_call x1, Pallas kernels, whole(): call(inverse_y, [shape(2, 64, N), shape(32, 8, 128)], specs + [VM], scrat...  2.01 us
    pallas_call x1, Pallas kernels, whole(): call(phases, (shape(2, NREF, QUART, 128), shape(2, NREF, QUART, 128), sha...  1.98 us
  transfers between devices with their start and end apart: 22, of which 5 were waited for; matrix products, arithmetic and copies ran while one was open for 0% of the time, Pallas kernels for 8%

profile of v1, /device:TPU:2, one launch (start us, length us, event | category | flops | bytes accessed | tf_op | source)
XLA Modules:
  0.0 65.3 jit_solution(12850408493417571262)
XLA Ops:
  0.6 0.0 copy-start.3
  0.6 0.0 copy-start.4
  0.7 0.0 copy-start.5
  0.7 0.0 copy-start.6
  0.7 2.6 %shard_map.141 = (f32[2,64,128]{2,1,0:T(8,128)}, f32[2,64,128]{2,1,0:T(8,128)}, f32[2,64,128]{2,1,0:T(8,128)}, f32[2,64,128]{2,1,0:T(8,128)}, f32[2,64,128]{2,1,...) custom-call(s32[1]{0:T(128)} %bitcast.pos_ref, f32[2,64,2,512]{3,2,1,0:T(2,128)} %wave_hbm.1, ...), custom_call_target="tpu_custom_call" | custom-call | tf_op jit(solution)/shard_map/pallas_call | solution.py:330
  3.3 2.2 %collective-permute-start = (f32[2,64,128]{2,1,0:T(8,128)}, f32[2,64,128]{2,1,0:T(8,128)S(1)}, u32[]{:S(2)}, u32[]{:S(2)}) collective-permute-start(f32[2,64,128]{2,1,0:T(8,128)} %get-tuple-element.36), channel_id=1, source_target_pairs={{0,4},{1,5},{2,6},{3,7},{4,0},{5,1},{6,2},{7,3},{8,12},{9,13},{10,... | collective-permute-start | bytes 196616 | tf_op jit(solution)/shard_map/ppermute | solution.py:323
  5.5 0.6 collective-permute-start.1
  6.1 1.5 %collective-permute-start.2 = (f32[2,64,128]{2,1,0:T(8,128)}, f32[2,64,128]{2,1,0:T(8,128)S(1)}, u32[]{:S(2)}, u32[]{:S(2)}) collective-permute-start(f32[2,64,128]{2,1,0:T(8,128)} %get-tuple-element.38), channel_id=1, source_target_pairs={{0,2},{1,3},{2,4},{3,5},{4,6},{5,7},{6,0},{7,1},{8,10},{9,11},{10,... | collective-permute-start | bytes 196616 | tf_op jit(solution)/shard_map/ppermute | solution.py:323
  7.6 1.5 %collective-permute-start.3 = (f32[2,64,128]{2,1,0:T(8,128)}, f32[2,64,128]{2,1,0:T(8,128)S(1)}, u32[]{:S(2)}, u32[]{:S(2)}) collective-permute-start(f32[2,64,128]{2,1,0:T(8,128)} %get-tuple-element.39), channel_id=1, source_target_pairs={{0,3},{1,2},{2,5},{3,4},{4,7},{5,6},{6,1},{7,0},{8,11},{9,10},{10,... | collective-permute-start | bytes 196616 | tf_op jit(solution)/shard_map/ppermute | solution.py:323
  9.1 0.8 %collective-permute-start.4 = (f32[2,64,128]{2,1,0:T(8,128)}, f32[2,64,128]{2,1,0:T(8,128)S(1)}, u32[]{:S(2)}, u32[]{:S(2)}) collective-permute-start(f32[2,64,128]{2,1,0:T(8,128)} %get-tuple-element.40), channel_id=1, source_target_pairs={{0,6},{1,7},{2,0},{3,1},{4,2},{5,3},{6,4},{7,5},{8,14},{9,15},{10,... | collective-permute-start | bytes 196616 | tf_op jit(solution)/shard_map/ppermute | solution.py:323
  9.9 0.0 collective-permute-done.refs_0_
  9.9 1.7 %collective-permute-start.5 = (f32[2,64,128]{2,1,0:T(8,128)}, f32[2,64,128]{2,1,0:T(8,128)S(1)}, u32[]{:S(2)}, u32[]{:S(2)}) collective-permute-start(f32[2,64,128]{2,1,0:T(8,128)} %get-tuple-element.41), channel_id=1, source_target_pairs={{0,7},{1,6},{2,1},{3,0},{4,3},{5,2},{6,5},{7,4},{8,15},{9,14},{10,... | collective-permute-start | bytes 196616 | tf_op jit(solution)/shard_map/ppermute | solution.py:323
  11.6 0.7 %collective-permute-start.6 = (f32[2,64,128]{2,1,0:T(8,128)}, f32[2,64,128]{2,1,0:T(8,128)S(1)}, u32[]{:S(2)}, u32[]{:S(2)}) collective-permute-start(f32[2,64,128]{2,1,0:T(8,128)} %get-tuple-element.42), channel_id=1, source_target_pairs={{0,1},{1,0},{2,3},{3,2},{4,5},{5,4},{6,7},{7,6},{8,9},{9,8},{10,11... | collective-permute-start | bytes 196616 | tf_op jit(solution)/shard_map/ppermute | solution.py:323
  12.3 2.0 %shard_map.140 = (f32[2,6,128,128]{3,2,1,0:T(8,128)S(1)}, f32[2,6,128,128]{3,2,1,0:T(8,128)S(1)}, f32[2,6,2,8,128]{4,3,2,1,0:T(8,128)S(1)}) custom-call(s32[1]{0:T(128)} %bitcast.pos_ref, f32[2]{0:T(128)S(1)} %copy-done.10, f32[6]{0:T(128)S(1)} %bitcast.6), custom_call_target="tpu_custom_call" | custom-call | tf_op jit(solution)/shard_map/pallas_call | solution.py:344
  14.3 0.0 copy-start.8
  14.3 0.0 collective-permute-done.2.refs_2_
  14.3 0.0 collective-permute-done.4.refs_4_
  14.3 0.2 collective-permute-done.5.refs_5_
  14.5 0.4 copy-done.8
  15.0 0.8 %copy-done.7 = f32[2,64,128]{2,1,0:T(8,128)S(1)} copy-done((f32[2,64,128]{2,1,0:T(8,128)S(1)}, f32[2,64,128]{2,1,0:T(8,128)}, u32[]{:S(2)}) %copy-start.7) | copy-done | bytes 65560
  15.8 1.5 %shard_map.142 = (f32[3,64,128]{2,1,0:T(8,128)S(1)}, f32[3,64,128]{2,1,0:T(8,128)S(1)}, f32[3,64,128]{2,1,0:T(8,128)S(1)}, f32[3,64,128]{2,1,0:T(8,128)S(1)}, f3...) custom-call(s32[1]{0:T(128)} %bitcast.pos_ref, ...), custom_call_target="tpu_custom_call" | custom-call | tf_op jit(solution)/shard_map/pallas_call | solution.py:349
  17.3 3.2 %collective-permute-start.7 = (f32[3,64,128]{2,1,0:T(8,128)S(1)}, f32[3,64,128]{2,1,0:T(8,128)S(1)}, u32[]{:S(2)}, u32[]{:S(2)}) collective-permute-start(f32[3,64,128]{2,1,0:T(8,128)S(1)} %get-tuple-element.44), channel_id=1, source_target_pairs={{0,4},{1,5},{2,6},{3,7},{4,0},{5,1},{6,2},{7,3},{8,12},{9,13},{10,... | collective-permute-start | bytes 294920 | tf_op jit(solution)/shard_map/ppermute | solution.py:323
  20.5 0.4 collective-permute-start.8
  20.9 0.8 %collective-permute-start.9 = (f32[3,64,128]{2,1,0:T(8,128)S(1)}, f32[3,64,128]{2,1,0:T(8,128)S(1)}, u32[]{:S(2)}, u32[]{:S(2)}) collective-permute-start(f32[3,64,128]{2,1,0:T(8,128)S(1)} %get-tuple-element.46), channel_id=1, source_target_pairs={{0,2},{1,3},{2,4},{3,5},{4,6},{5,7},{6,0},{7,1},{8,10},{9,11},{10,... | collective-permute-start | bytes 294920 | tf_op jit(solution)/shard_map/ppermute | solution.py:323
  21.7 2.4 %collective-permute-start.10 = (f32[3,64,128]{2,1,0:T(8,128)S(1)}, f32[3,64,128]{2,1,0:T(8,128)S(1)}, u32[]{:S(2)}, u32[]{:S(2)}) collective-permute-start(f32[3,64,128]{2,1,0:T(8,128)S(1)} %get-tuple-element.47), channel_id=1, source_target_pairs={{0,3},{1,2},{2,5},{3,4},{4,7},{5,6},{6,1},{7,0},{8,11},{9,10},{10,... | collective-permute-start | bytes 294920 | tf_op jit(solution)/shard_map/ppermute | solution.py:323
  24.0 0.0 collective-permute-start.11
  24.1 1.5 %shard_map.144 = (f32[3,64,128]{2,1,0:T(8,128)S(1)}, f32[3,64,128]{2,1,0:T(8,128)S(1)}, f32[3,64,128]{2,1,0:T(8,128)S(1)}, f32[3,64,128]{2,1,0:T(8,128)S(1)}, f3...) custom-call(s32[1]{0:T(128)} %bitcast.pos_ref, ...), custom_call_target="tpu_custom_call" | custom-call | tf_op jit(solution)/shard_map/pallas_call | solution.py:349
  25.6 1.6 %collective-permute-start.12 = (f32[3,64,128]{2,1,0:T(8,128)S(1)}, f32[3,64,128]{2,1,0:T(8,128)S(1)}, u32[]{:S(2)}, u32[]{:S(2)}) collective-permute-start(f32[3,64,128]{2,1,0:T(8,128)S(1)} %get-tuple-element.49), channel_id=1, source_target_pairs={{0,7},{1,6},{2,1},{3,0},{4,3},{5,2},{6,5},{7,4},{8,15},{9,14},{10,... | collective-permute-start | bytes 294920 | tf_op jit(solution)/shard_map/ppermute | solution.py:323
  27.1 0.0 collective-permute-done.8.refs_1_
  27.1 0.7 %collective-permute-start.13 = (f32[3,64,128]{2,1,0:T(8,128)S(1)}, f32[3,64,128]{2,1,0:T(8,128)S(1)}, u32[]{:S(2)}, u32[]{:S(2)}) collective-permute-start(f32[3,64,128]{2,1,0:T(8,128)S(1)} %get-tuple-element.50), channel_id=1, source_target_pairs={{0,1},{1,0},{2,3},{3,2},{4,5},{5,4},{6,7},{7,6},{8,9},{9,8},{10,11... | collective-permute-start | bytes 294920 | tf_op jit(solution)/shard_map/ppermute | solution.py:323
  27.8 0.6 collective-permute-done.9.refs_2_
  28.4 1.6 %collective-permute-start.14 = (f32[3,64,128]{2,1,0:T(8,128)S(1)}, f32[3,64,128]{2,1,0:T(8,128)S(1)}, u32[]{:S(2)}, u32[]{:S(2)}) collective-permute-start(f32[3,64,128]{2,1,0:T(8,128)S(1)} %get-tuple-element.53), channel_id=1, source_target_pairs={{0,4},{1,5},{2,6},{3,7},{4,0},{5,1},{6,2},{7,3},{8,12},{9,13},{10,... | collective-permute-start | bytes 294920 | tf_op jit(solution)/shard_map/ppermute | solution.py:323
  30.0 0.0 collective-permute-done.10.refs_3_
  30.0 1.1 %collective-permute-start.15 = (f32[3,64,128]{2,1,0:T(8,128)S(1)}, f32[3,64,128]{2,1,0:T(8,128)S(1)}, u32[]{:S(2)}, u32[]{:S(2)}) collective-permute-start(f32[3,64,128]{2,1,0:T(8,128)S(1)} %get-tuple-element.54), channel_id=1, source_target_pairs={{0,5},{1,4},{2,7},{3,6},{4,1},{5,0},{6,3},{7,2},{8,13},{9,12},{10,... | collective-permute-start | bytes 294920 | tf_op jit(solution)/shard_map/ppermute | solution.py:323
  31.1 2.3 %collective-permute-start.16 = (f32[3,64,128]{2,1,0:T(8,128)S(1)}, f32[3,64,128]{2,1,0:T(8,128)S(1)}, u32[]{:S(2)}, u32[]{:S(2)}) collective-permute-start(f32[3,64,128]{2,1,0:T(8,128)S(1)} %get-tuple-element.55), channel_id=1, source_target_pairs={{0,2},{1,3},{2,4},{3,5},{4,6},{5,7},{6,0},{7,1},{8,10},{9,11},{10,... | collective-permute-start | bytes 294920 | tf_op jit(solution)/shard_map/ppermute | solution.py:323
  33.4 0.1 collective-permute-start.17
  33.5 1.6 %collective-permute-start.18 = (f32[3,64,128]{2,1,0:T(8,128)S(1)}, f32[3,64,128]{2,1,0:T(8,128)S(1)}, u32[]{:S(2)}, u32[]{:S(2)}) collective-permute-start(f32[3,64,128]{2,1,0:T(8,128)S(1)} %get-tuple-element.57), channel_id=1, source_target_pairs={{0,6},{1,7},{2,0},{3,1},{4,2},{5,3},{6,4},{7,5},{8,14},{9,15},{10,... | collective-permute-start | bytes 294920 | tf_op jit(solution)/shard_map/ppermute | solution.py:323
  35.1 1.1 %collective-permute-start.19 = (f32[3,64,128]{2,1,0:T(8,128)S(1)}, f32[3,64,128]{2,1,0:T(8,128)S(1)}, u32[]{:S(2)}, u32[]{:S(2)}) collective-permute-start(f32[3,64,128]{2,1,0:T(8,128)S(1)} %get-tuple-element.58), channel_id=1, source_target_pairs={{0,7},{1,6},{2,1},{3,0},{4,3},{5,2},{6,5},{7,4},{8,15},{9,14},{10,... | collective-permute-start | bytes 294920 | tf_op jit(solution)/shard_map/ppermute | solution.py:323
  36.3 0.0 collective-permute-done.15.refs_1_
  36.3 0.7 %collective-permute-start.20 = (f32[3,64,128]{2,1,0:T(8,128)S(1)}, f32[3,64,128]{2,1,0:T(8,128)S(1)}, u32[]{:S(2)}, u32[]{:S(2)}) collective-permute-start(f32[3,64,128]{2,1,0:T(8,128)S(1)} %get-tuple-element.59), channel_id=1, source_target_pairs={{0,1},{1,0},{2,3},{3,2},{4,5},{5,4},{6,7},{7,6},{8,9},{9,8},{10,11... | collective-permute-start | bytes 294920 | tf_op jit(solution)/shard_map/ppermute | solution.py:323
  37.0 1.1 %shard_map.143 = (f32[2,64,512]{2,1,0:T(8,128)S(1)}, f32[64,512]{1,0:T(8,128)S(1)}) custom-call(s32[1]{0:T(128)} %bitcast.pos_ref, s32[1,8,8]{2,1,0:T(8,128)S(1)} %copy-done.8, f32[1,8,8]{2,1,0:T(8,128)S(1)} %copy-done.9, f32[2,64,2,512]{3,2,1,0:T(2,128)S(1)} %bitcast.4, bf16[2,256,256]{2,1,0:T(8,128)(2,1)S(1)} %copy-done, ...), custom_call_target="tpu_custom_call" | custom-call | tf_op jit(solution)/shard_map/pallas_call | solution.py:367
  38.0 0.8 %collective-permute-done.16.refs_2_ = f32[3,64,128]{2,1,0:T(8,128)S(1)} collective-permute-done((f32[3,64,128]{2,1,0:T(8,128)S(1)}, f32[3,64,128]{2,1,0:T(8,128)S(1)}, u32[]{:S(2)}, u32[]{:S(2)}) %collective-permute-start.16) | collective-permute-done | bytes 98336 | tf_op jit(solution)/shard_map/ppermute | solution.py:323
  38.9 2.2 %collective-permute-done.17.refs_3_ = f32[3,64,128]{2,1,0:T(8,128)S(1)} collective-permute-done((f32[3,64,128]{2,1,0:T(8,128)S(1)}, f32[3,64,128]{2,1,0:T(8,128)S(1)}, u32[]{:S(2)}, u32[]{:S(2)}) %collective-permute-start.17) | collective-permute-done | bytes 98336 | tf_op jit(solution)/shard_map/ppermute | solution.py:323
  41.0 2.0 %shard_map.145 = (f32[2,64,512]{2,1,0:T(8,128)S(1)}, f32[32,8,128]{2,1,0:T(8,128)}) custom-call(s32[1]{0:T(128)} %bitcast.pos_ref, s32[1,8,8]{2,1,0:T(8,128)S(1)} %copy-done.8, f32[1,8,8]{2,1,0:T(8,128)S(1)} %copy-done.9, f32[2,64,2,512]{3,2,1,0:T(2,128)S(1)} %bitcast.5, bf16[2,256,256]{2,1,0:T(8,128)(2,1)S(1)} %copy-done, ...), custom_call_target="tpu_custom_call" | custom-call | tf_op jit(solution)/shard_map/pallas_call | solution.py:368
  43.1 10.9 %all-to-all-start = ((f32[32,8,128]{2,1,0:T(8,128)}), f32[32,8,128]{2,1,0:T(8,128)S(1)}, u32[]{:S(2)}, u32[]{:S(2)}) async-start(f32[32,8,128]{2,1,0:T(8,128)} %get-tuple-element.63), calls=%async_computation | async-start | bytes 262144 | tf_op jit(solution)/shard_map/all_to_all | solution.py:375
  53.9 0.9 %shard_map.146 = f32[2,64,2,512]{3,2,1,0:T(2,128)} custom-call(f32[2,64,512]{2,1,0:T(8,128)S(1)} %get-tuple-element.52.first_ref, f32[2,64,512]{2,1,0:T(8,128)S(1)} %get-tuple-element.62.second_ref), custom_call_target="tpu_custom_call" | custom-call | tf_op jit(solution)/shard_map/pallas_call | solution.py:376
  54.8 9.7 %all-to-all-done.came_ref = f32[32,8,128]{2,1,0:T(8,128)S(1)} async-done(((f32[32,8,128]{2,1,0:T(8,128)}), f32[32,8,128]{2,1,0:T(8,128)S(1)}, u32[]{:S(2)}, u32[]{:S(2)}) %all-to-all-start) | async-done | bytes 131104 | tf_op jit(solution)/shard_map/all_to_all | solution.py:375
  64.5 0.8 %shard_map.147 = f32[1,16,64]{2,1,0:T(8,128)} custom-call(f32[32,8,128]{2,1,0:T(8,128)S(1)} %all-to-all-done.came_ref), custom_call_target="tpu_custom_call" | custom-call | tf_op jit(solution)/shard_map/pallas_call | solution.py:377
  (28 shorter events, 0.1 us)
Async XLA Ops:
  0.6 13.9 %copy-start.3 = (bf16[2,256,256]{2,1,0:T(8,128)(2,1)S(1)}, bf16[2,256,256]{2,1,0:T(8,128)(2,1)}, u32[]{:S(2)}) copy-start(bf16[2,256,256]{2,1,0:T(8,128)(2,1)} %constant.21.clone.ae_ref) | copy-start | bytes 786436
  0.6 13.9 %copy-start.4 = (bf16[2,256,256]{2,1,0:T(8,128)(2,1)S(1)}, bf16[2,256,256]{2,1,0:T(8,128)(2,1)}, u32[]{:S(2)}) copy-start(bf16[2,256,256]{2,1,0:T(8,128)(2,1)} %constant.22.clone.ao_ref) | copy-start | bytes 786436
  0.7 13.9 %copy-start.5 = (bf16[2,256,256]{2,1,0:T(8,128)(2,1)S(1)}, bf16[2,256,256]{2,1,0:T(8,128)(2,1)}, u32[]{:S(2)}) copy-start(bf16[2,256,256]{2,1,0:T(8,128)(2,1)} %constant.23.clone.be_ref) | copy-start | bytes 786436
  0.7 13.9 %copy-start.6 = (bf16[2,256,256]{2,1,0:T(8,128)(2,1)S(1)}, bf16[2,256,256]{2,1,0:T(8,128)(2,1)}, u32[]{:S(2)}) copy-start(bf16[2,256,256]{2,1,0:T(8,128)(2,1)} %constant.24.clone.bo_ref) | copy-start | bytes 786436
  3.3 6.6 %collective-permute-start = (f32[2,64,128]{2,1,0:T(8,128)}, f32[2,64,128]{2,1,0:T(8,128)S(1)}, u32[]{:S(2)}, u32[]{:S(2)}) collective-permute-start(f32[2,64,128]{2,1,0:T(8,128)} %get-tuple-element.36), channel_id=1, source_target_pairs={{0,4},{1,5},{2,6},{3,7},{4,0},{5,1},{6,2},{7,3},{8,12},{9,13},{10,... | collective-permute-start | bytes 196616 | tf_op jit(solution)/shard_map/ppermute | solution.py:323
  5.5 6.1 %collective-permute-start.1 = (f32[2,64,128]{2,1,0:T(8,128)}, f32[2,64,128]{2,1,0:T(8,128)S(1)}, u32[]{:S(2)}, u32[]{:S(2)}) collective-permute-start(f32[2,64,128]{2,1,0:T(8,128)} %get-tuple-element.37), channel_id=1, source_target_pairs={{0,5},{1,4},{2,7},{3,6},{4,1},{5,0},{6,3},{7,2},{8,13},{9,12},{10,... | collective-permute-start | bytes 196616 | tf_op jit(solution)/shard_map/ppermute | solution.py:323
  6.1 8.2 %collective-permute-start.2 = (f32[2,64,128]{2,1,0:T(8,128)}, f32[2,64,128]{2,1,0:T(8,128)S(1)}, u32[]{:S(2)}, u32[]{:S(2)}) collective-permute-start(f32[2,64,128]{2,1,0:T(8,128)} %get-tuple-element.38), channel_id=1, source_target_pairs={{0,2},{1,3},{2,4},{3,5},{4,6},{5,7},{6,0},{7,1},{8,10},{9,11},{10,... | collective-permute-start | bytes 196616 | tf_op jit(solution)/shard_map/ppermute | solution.py:323
  7.6 6.7 %collective-permute-start.3 = (f32[2,64,128]{2,1,0:T(8,128)}, f32[2,64,128]{2,1,0:T(8,128)S(1)}, u32[]{:S(2)}, u32[]{:S(2)}) collective-permute-start(f32[2,64,128]{2,1,0:T(8,128)} %get-tuple-element.39), channel_id=1, source_target_pairs={{0,3},{1,2},{2,5},{3,4},{4,7},{5,6},{6,1},{7,0},{8,11},{9,10},{10,... | collective-permute-start | bytes 196616 | tf_op jit(solution)/shard_map/ppermute | solution.py:323
  9.1 5.2 %collective-permute-start.4 = (f32[2,64,128]{2,1,0:T(8,128)}, f32[2,64,128]{2,1,0:T(8,128)S(1)}, u32[]{:S(2)}, u32[]{:S(2)}) collective-permute-start(f32[2,64,128]{2,1,0:T(8,128)} %get-tuple-element.40), channel_id=1, source_target_pairs={{0,6},{1,7},{2,0},{3,1},{4,2},{5,3},{6,4},{7,5},{8,14},{9,15},{10,... | collective-permute-start | bytes 196616 | tf_op jit(solution)/shard_map/ppermute | solution.py:323
  9.9 4.6 %collective-permute-start.5 = (f32[2,64,128]{2,1,0:T(8,128)}, f32[2,64,128]{2,1,0:T(8,128)S(1)}, u32[]{:S(2)}, u32[]{:S(2)}) collective-permute-start(f32[2,64,128]{2,1,0:T(8,128)} %get-tuple-element.41), channel_id=1, source_target_pairs={{0,7},{1,6},{2,1},{3,0},{4,3},{5,2},{6,5},{7,4},{8,15},{9,14},{10,... | collective-permute-start | bytes 196616 | tf_op jit(solution)/shard_map/ppermute | solution.py:323
  11.6 0.7 %copy-start.10 = (f32[2]{0:T(128)S(1)}, f32[2]{0:T(128)}, u32[]{:S(2)}) copy-start(f32[2]{0:T(128)} %omega_ref.1) | copy-start | bytes 28
  11.6 0.7 %copy-start.11 = (f32[1,6]{1,0:T(1,128)S(1)}, f32[1,6]{1,0:T(1,128)}, u32[]{:S(2)}) copy-start(f32[1,6]{1,0:T(1,128)} %param.16) | copy-start | bytes 76
  11.6 2.9 %collective-permute-start.6 = (f32[2,64,128]{2,1,0:T(8,128)}, f32[2,64,128]{2,1,0:T(8,128)S(1)}, u32[]{:S(2)}, u32[]{:S(2)}) collective-permute-start(f32[2,64,128]{2,1,0:T(8,128)} %get-tuple-element.42), channel_id=1, source_target_pairs={{0,1},{1,0},{2,3},{3,2},{4,5},{5,4},{6,7},{7,6},{8,9},{9,8},{10,11... | collective-permute-start | bytes 196616 | tf_op jit(solution)/shard_map/ppermute | solution.py:323
  14.3 0.7 %copy-start.8 = (s32[1,8,8]{2,1,0:T(8,128)S(1)}, s32[1,8,8]{2,1,0:T(8,128)}, u32[]{:S(2)}) copy-start(s32[1,8,8]{2,1,0:T(8,128)} %lower_hbm.7) | copy-start | bytes 772
  14.9 0.8 %copy-start.7 = (f32[2,64,128]{2,1,0:T(8,128)S(1)}, f32[2,64,128]{2,1,0:T(8,128)}, u32[]{:S(2)}) copy-start(f32[2,64,128]{2,1,0:T(8,128)} %get-tuple-element.43.refs_7_) | copy-start | bytes 196612
  17.3 8.3 %collective-permute-start.7 = (f32[3,64,128]{2,1,0:T(8,128)S(1)}, f32[3,64,128]{2,1,0:T(8,128)S(1)}, u32[]{:S(2)}, u32[]{:S(2)}) collective-permute-start(f32[3,64,128]{2,1,0:T(8,128)S(1)} %get-tuple-element.44), channel_id=1, source_target_pairs={{0,4},{1,5},{2,6},{3,7},{4,0},{5,1},{6,2},{7,3},{8,12},{9,13},{10,... | collective-permute-start | bytes 294920 | tf_op jit(solution)/shard_map/ppermute | solution.py:323
  20.5 6.6 %collective-permute-start.8 = (f32[3,64,128]{2,1,0:T(8,128)S(1)}, f32[3,64,128]{2,1,0:T(8,128)S(1)}, u32[]{:S(2)}, u32[]{:S(2)}) collective-permute-start(f32[3,64,128]{2,1,0:T(8,128)S(1)} %get-tuple-element.45), channel_id=1, source_target_pairs={{0,5},{1,4},{2,7},{3,6},{4,1},{5,0},{6,3},{7,2},{8,13},{9,12},{10,... | collective-permute-start | bytes 294920 | tf_op jit(solution)/shard_map/ppermute | solution.py:323
  20.9 7.5 %collective-permute-start.9 = (f32[3,64,128]{2,1,0:T(8,128)S(1)}, f32[3,64,128]{2,1,0:T(8,128)S(1)}, u32[]{:S(2)}, u32[]{:S(2)}) collective-permute-start(f32[3,64,128]{2,1,0:T(8,128)S(1)} %get-tuple-element.46), channel_id=1, source_target_pairs={{0,2},{1,3},{2,4},{3,5},{4,6},{5,7},{6,0},{7,1},{8,10},{9,11},{10,... | collective-permute-start | bytes 294920 | tf_op jit(solution)/shard_map/ppermute | solution.py:323
  21.7 8.3 %collective-permute-start.10 = (f32[3,64,128]{2,1,0:T(8,128)S(1)}, f32[3,64,128]{2,1,0:T(8,128)S(1)}, u32[]{:S(2)}, u32[]{:S(2)}) collective-permute-start(f32[3,64,128]{2,1,0:T(8,128)S(1)} %get-tuple-element.47), channel_id=1, source_target_pairs={{0,3},{1,2},{2,5},{3,4},{4,7},{5,6},{6,1},{7,0},{8,11},{9,10},{10,... | collective-permute-start | bytes 294920 | tf_op jit(solution)/shard_map/ppermute | solution.py:323
  24.0 12.9 %copy-start = (bf16[2,256,256]{2,1,0:T(8,128)(2,1)S(1)}, bf16[2,256,256]{2,1,0:T(8,128)(2,1)}, u32[]{:S(2)}) copy-start(bf16[2,256,256]{2,1,0:T(8,128)(2,1)} %constant.18.clone.even_hbm.even_ref) | copy-start | bytes 786436
  24.0 12.9 %copy-start.1 = (f32[1,2,64,2,512]{4,3,2,1,0:T(2,128)S(1)}, f32[1,2,64,2,512]{4,3,2,1,0:T(2,128)}, u32[]{:S(2)}) copy-start(f32[1,2,64,2,512]{4,3,2,1,0:T(2,128)} %param.14) | copy-start | bytes 1572868
  24.0 12.9 %copy-start.2 = (bf16[2,256,256]{2,1,0:T(8,128)(2,1)S(1)}, bf16[2,256,256]{2,1,0:T(8,128)(2,1)}, u32[]{:S(2)}) copy-start(bf16[2,256,256]{2,1,0:T(8,128)(2,1)} %constant.20.clone.odd_ref) | copy-start | bytes 786436
  24.0 7.0 %collective-permute-start.11 = (f32[3,64,128]{2,1,0:T(8,128)S(1)}, f32[3,64,128]{2,1,0:T(8,128)S(1)}, u32[]{:S(2)}, u32[]{:S(2)}) collective-permute-start(f32[3,64,128]{2,1,0:T(8,128)S(1)} %get-tuple-element.48), channel_id=1, source_target_pairs={{0,6},{1,7},{2,0},{3,1},{4,2},{5,3},{6,4},{7,5},{8,14},{9,15},{10,... | collective-permute-start | bytes 294920 | tf_op jit(solution)/shard_map/ppermute | solution.py:323
  25.6 7.8 %collective-permute-start.12 = (f32[3,64,128]{2,1,0:T(8,128)S(1)}, f32[3,64,128]{2,1,0:T(8,128)S(1)}, u32[]{:S(2)}, u32[]{:S(2)}) collective-permute-start(f32[3,64,128]{2,1,0:T(8,128)S(1)} %get-tuple-element.49), channel_id=1, source_target_pairs={{0,7},{1,6},{2,1},{3,0},{4,3},{5,2},{6,5},{7,4},{8,15},{9,14},{10,... | collective-permute-start | bytes 294920 | tf_op jit(solution)/shard_map/ppermute | solution.py:323
  27.1 6.4 %collective-permute-start.13 = (f32[3,64,128]{2,1,0:T(8,128)S(1)}, f32[3,64,128]{2,1,0:T(8,128)S(1)}, u32[]{:S(2)}, u32[]{:S(2)}) collective-permute-start(f32[3,64,128]{2,1,0:T(8,128)S(1)} %get-tuple-element.50), channel_id=1, source_target_pairs={{0,1},{1,0},{2,3},{3,2},{4,5},{5,4},{6,7},{7,6},{8,9},{9,8},{10,11... | collective-permute-start | bytes 294920 | tf_op jit(solution)/shard_map/ppermute | solution.py:323
  28.4 6.8 %collective-permute-start.14 = (f32[3,64,128]{2,1,0:T(8,128)S(1)}, f32[3,64,128]{2,1,0:T(8,128)S(1)}, u32[]{:S(2)}, u32[]{:S(2)}) collective-permute-start(f32[3,64,128]{2,1,0:T(8,128)S(1)} %get-tuple-element.53), channel_id=1, source_target_pairs={{0,4},{1,5},{2,6},{3,7},{4,0},{5,1},{6,2},{7,3},{8,12},{9,13},{10,... | collective-permute-start | bytes 294920 | tf_op jit(solution)/shard_map/ppermute | solution.py:323
  30.0 6.3 %collective-permute-start.15 = (f32[3,64,128]{2,1,0:T(8,128)S(1)}, f32[3,64,128]{2,1,0:T(8,128)S(1)}, u32[]{:S(2)}, u32[]{:S(2)}) collective-permute-start(f32[3,64,128]{2,1,0:T(8,128)S(1)} %get-tuple-element.54), channel_id=1, source_target_pairs={{0,5},{1,4},{2,7},{3,6},{4,1},{5,0},{6,3},{7,2},{8,13},{9,12},{10,... | collective-permute-start | bytes 294920 | tf_op jit(solution)/shard_map/ppermute | solution.py:323
  31.1 7.8 %collective-permute-start.16 = (f32[3,64,128]{2,1,0:T(8,128)S(1)}, f32[3,64,128]{2,1,0:T(8,128)S(1)}, u32[]{:S(2)}, u32[]{:S(2)}) collective-permute-start(f32[3,64,128]{2,1,0:T(8,128)S(1)} %get-tuple-element.55), channel_id=1, source_target_pairs={{0,2},{1,3},{2,4},{3,5},{4,6},{5,7},{6,0},{7,1},{8,10},{9,11},{10,... | collective-permute-start | bytes 294920 | tf_op jit(solution)/shard_map/ppermute | solution.py:323
  33.4 7.6 %collective-permute-start.17 = (f32[3,64,128]{2,1,0:T(8,128)S(1)}, f32[3,64,128]{2,1,0:T(8,128)S(1)}, u32[]{:S(2)}, u32[]{:S(2)}) collective-permute-start(f32[3,64,128]{2,1,0:T(8,128)S(1)} %get-tuple-element.56), channel_id=1, source_target_pairs={{0,3},{1,2},{2,5},{3,4},{4,7},{5,6},{6,1},{7,0},{8,11},{9,10},{10,... | collective-permute-start | bytes 294920 | tf_op jit(solution)/shard_map/ppermute | solution.py:323
  33.5 3.4 %copy-start.9 = (f32[1,8,8]{2,1,0:T(8,128)S(1)}, f32[1,8,8]{2,1,0:T(8,128)}, u32[]{:S(2)}) copy-start(f32[1,8,8]{2,1,0:T(8,128)} %weight_hbm.3) | copy-start | bytes 772
  33.5 7.5 %collective-permute-start.18 = (f32[3,64,128]{2,1,0:T(8,128)S(1)}, f32[3,64,128]{2,1,0:T(8,128)S(1)}, u32[]{:S(2)}, u32[]{:S(2)}) collective-permute-start(f32[3,64,128]{2,1,0:T(8,128)S(1)} %get-tuple-element.57), channel_id=1, source_target_pairs={{0,6},{1,7},{2,0},{3,1},{4,2},{5,3},{6,4},{7,5},{8,14},{9,15},{10,... | collective-permute-start | bytes 294920 | tf_op jit(solution)/shard_map/ppermute | solution.py:323
  35.1 5.9 %collective-permute-start.19 = (f32[3,64,128]{2,1,0:T(8,128)S(1)}, f32[3,64,128]{2,1,0:T(8,128)S(1)}, u32[]{:S(2)}, u32[]{:S(2)}) collective-permute-start(f32[3,64,128]{2,1,0:T(8,128)S(1)} %get-tuple-element.58), channel_id=1, source_target_pairs={{0,7},{1,6},{2,1},{3,0},{4,3},{5,2},{6,5},{7,4},{8,15},{9,14},{10,... | collective-permute-start | bytes 294920 | tf_op jit(solution)/shard_map/ppermute | solution.py:323
  36.3 4.8 %collective-permute-start.20 = (f32[3,64,128]{2,1,0:T(8,128)S(1)}, f32[3,64,128]{2,1,0:T(8,128)S(1)}, u32[]{:S(2)}, u32[]{:S(2)}) collective-permute-start(f32[3,64,128]{2,1,0:T(8,128)S(1)} %get-tuple-element.59), channel_id=1, source_target_pairs={{0,1},{1,0},{2,3},{3,2},{4,5},{5,4},{6,7},{7,6},{8,9},{9,8},{10,11... | collective-permute-start | bytes 294920 | tf_op jit(solution)/shard_map/ppermute | solution.py:323
  43.1 21.5 %all-to-all-start = ((f32[32,8,128]{2,1,0:T(8,128)}), f32[32,8,128]{2,1,0:T(8,128)S(1)}, u32[]{:S(2)}, u32[]{:S(2)}) async-start(f32[32,8,128]{2,1,0:T(8,128)} %get-tuple-element.63), calls=%async_computation | async-start | bytes 262144 | tf_op jit(solution)/shard_map/all_to_all | solution.py:375

commit v2 on v0

v2 whole, which is shorter than its diff:
```python
import functools
import math

import jax
import jax.numpy as jnp
import numpy as np
from jax import lax
from jax.experimental import pallas as pl
from jax.experimental.pallas import tpu as pltpu
from jax.sharding import PartitionSpec as P


N = 512
NREF = 6
NEED = 3
STEP = 10.0
UNIT = 2.0 * math.pi / (N * 12.5)
HALF = N // 2
QUART = N // 4
BF = jnp.bfloat16
F32 = jnp.float32
INTERPRET = False
FIRST = 60


def split(values):
    high = values.astype(BF)
    return high, (values - high.astype(F32)).astype(BF)


def tables():
    place = np.arange(HALF)
    cas = lambda k: (lambda t: np.cos(t) + np.sin(t))((place[:, None] * k[None, :] % N) * (2.0 * np.pi / N)) / np.sqrt(N)
    j = np.arange(QUART)
    fold_even = cas(np.concatenate([2 * j, [HALF], N - 2 * j[1:]]))
    fold_odd = cas(np.concatenate([2 * j + 1, N - 1 - 2 * j]))
    out = []
    for stack in ((fold_even, fold_odd), (fold_even.T, fold_odd.T)):
        table = np.stack(stack)
        high = np.asarray(table, np.float32).astype(jnp.bfloat16)
        low = (table - high.astype(np.float64)).astype(np.float32).astype(jnp.bfloat16)
        out.append(np.stack([high, low], axis=1))
    return out


def dot3(left, right):
    high = jnp.dot(jnp.concatenate(left, axis=0), right[0], preferred_element_type=F32)
    low = jnp.dot(left[0], right[1], preferred_element_type=F32)
    count = left[0].shape[0]
    return high[:count] + (high[count:] + low)


def low_lanes(shape):
    return lax.broadcasted_iota(jnp.int32, shape, len(shape) - 1) < 64


def forward_y(pos_ref, wave_hbm, table_hbm, own_ref, other_ref, wave_ref, table_ref, sem):
    pairs = ((wave_hbm, wave_ref), (table_hbm, table_ref))
    copies = [pltpu.make_async_copy(src, dst, sem.at[i]) for i, (src, dst) in enumerate(pairs)]
    for copy in copies:
        copy.start()
    for copy in copies:
        copy.wait()
    rows = jnp.concatenate([wave_ref[f, :, c, :] for f in range(2) for c in range(2)], axis=0)
    near, far = rows[:, :HALF], rows[:, HALF:]
    core = pos_ref[0] % 2
    for kind, out_ref in ((core, own_ref), (1 - core, other_ref)):
        mixed = near + far * (1 - 2 * kind).astype(F32)
        spectrum = dot3(split(mixed), (table_ref[kind, 0], table_ref[kind, 1]))
        for f in range(2):
            for c in range(2):
                start = 128 * f + 64 * c
                out_ref[f, :, HALF * c : HALF * c + HALF] = spectrum[start : start + 64]


def phase_of(q):
    root = jnp.sqrt(jnp.abs(q)) * STEP
    u = jnp.maximum(q, 0.0) * (STEP * STEP)
    cosine = jnp.full_like(u, -1.0 / math.factorial(14))
    for k in range(6, -1, -1):
        cosine = cosine * u + (-1.0) ** k / math.factorial(2 * k)
    sine = jnp.full_like(u, 1.0 / math.factorial(13))
    for k in range(5, -1, -1):
        sine = sine * u + (-1.0) ** k / math.factorial(2 * k + 1)
    damping = jnp.exp(-root)
    moving = q > 0.0
    return jnp.where(moving, cosine, damping), jnp.where(moving, sine * root, 0.0)


def rows_of(pos, i):
    return pos + i * (1 - 2 * (pos % 2))


def phases(f, pos_ref, lower_ref, omega_ref, speed_ref, cos_ref, sin_ref, nyq_ref, edge):
    lane = lax.broadcasted_iota(jnp.int32, (QUART, 128), 1)
    row = lax.broadcasted_iota(jnp.int32, (QUART, 128), 0)
    pos = pos_ref[0]
    core = pos % 2
    number = lambda values: values.astype(F32) * UNIT
    ky = number(2 * lane + core)
    ky2 = ky * ky
    bases = [base_of(lower_ref, rows_of(pos, i)) for i in range(2)]
    fix = lane == 128 * core

    def square(t):
        ratio = omega_ref[f] / speed_ref[jnp.where(t < NEED, bases[0] + t, bases[1] + t - NEED)]
        return ratio * ratio

    squares = jnp.zeros((QUART, 128), F32)
    for t in range(2 * NEED):
        squares = jnp.where(lane // 2 == t, square(t), squares)
    kx = number(2 * row + lane % 2)
    edge[0], edge[1] = phase_of(squares - (kx * kx + (HALF * UNIT) ** 2))

    def one(t, carry):
        now = square(t)
        for kind in range(2):
            kx = number(2 * row + kind)
            turn = (128 - 2 * t - kind) % 128
            for k, (ref, part) in enumerate(zip((cos_ref, sin_ref), phase_of(now - (kx * kx + ky2)))):
                ref[t, kind, :, :128] = part
                ref[t, kind, :, 128:] = jnp.where(fix, pltpu.roll(edge[k], turn, 1), part)
        for half in range(2):
            line = jnp.where(fix[:8], (HALF * UNIT) ** 2, ky2[:8]) if half else ky2[:8]
            for k, part in enumerate(phase_of(now - ((HALF * UNIT) ** 2 + line))):
                nyq_ref[t, k, :, 128 * half : 128 * half + 128] = part
        return carry

    lax.fori_loop(0, 2 * NEED, one, 0)


def shift_x(f, pos_ref, here_ref, right_ref, left_ref, far0_ref, far1_ref, cos_ref, sin_ref, nyq_ref, a_ref, b_ref, own_ref, other_ref, wave, spec):
    pos = pos_ref[0]
    chip, core = pos // 2, pos % 2
    sign = lambda flag: jnp.where(flag, 1.0, -1.0).astype(F32)
    mine = sign(chip < 2)
    theirs = sign((chip == 1) | (chip == 2))
    across = (far0_ref, far1_ref)
    for i in range(2):
        half = 64 * ((core + i) % 2)
        rows = pl.ds(pl.multiple_of(128 * (chip % 2) + half, 64), 64)
        a, b = here_ref[i], across[i][...]
        wave[0, rows, :] = a + b
        wave[1, rows, :] = (a - b) * mine
        rows = pl.ds(pl.multiple_of(128 * ((chip + 1) % 2) + half, 64), 64)
        a, b = right_ref[i], left_ref[i]
        wave[0, rows, :] = a + b
        wave[1, rows, :] = (a - b) * theirs
    for kind in range(2):
        spec[kind] = dot3((a_ref[kind, 0], a_ref[kind, 1]), split(wave[kind]))
    top = lax.broadcasted_iota(jnp.int32, (8, HALF), 0) == 0

    def one(j, carry):
        for i, out_ref in enumerate((own_ref, other_ref)):
            t = NEED * i + j
            p = rows_of(pos, i)
            rows = pl.ds(pl.multiple_of(64 * (p % 4), 64), 64)
            total = None
            for kind in range(2):
                c = cos_ref[t, kind]
                s = sin_ref[t, kind]
                pieces = []
                for block in range(2):
                    cc, ss = c, s
                    if kind == 0 and block == 1:
                        cc = jnp.concatenate([jnp.where(top, nyq_ref[t, 0], c[:8]), c[8:]], axis=0)
                        ss = jnp.concatenate([jnp.where(top, nyq_ref[t, 1], s[:8]), s[8:]], axis=0)
                    lines = slice(QUART * block, QUART * block + QUART)
                    re, im = spec[kind, lines, :HALF], spec[kind, lines, HALF:]
                    pieces.append(jnp.concatenate([re * cc - im * ss, re * ss + im * cc], axis=1))
                part = dot3((b_ref[kind, 0, rows, :], b_ref[kind, 1, rows, :]), split(jnp.concatenate(pieces, axis=0)))
                total = part if kind == 0 else total + part * sign(p < 4)
            out_ref[j] = total
        return carry

    for j in range(NEED):
        one(j, 0)


def base_of(lower_ref, p):
    base = lower_ref[p, 0]
    for q in range(1, 8):
        base = jnp.minimum(base, lower_ref[p, q])
    return jnp.minimum(base, NREF - NEED)


def inverse_y(f, pos_ref, lower_ref, weight_ref, source_ref, table_ref, own_ref, came_ref, *refs):
    pos = pos_ref[0]
    core = pos % 2
    halves = []
    for kind, ref in ((core, own_ref), (1 - core, came_ref)):
        rows = [ref[j, :, HALF * c : HALF * c + HALF] for j in range(NEED) for c in range(2)]
        halves.append(dot3(split(jnp.concatenate(rows, axis=0)), (table_ref[kind, 0], table_ref[kind, 1])))
    flip = (1 - 2 * core).astype(F32)
    base = base_of(lower_ref, pos)
    lane = low_lanes((1, 128))
    coef = []
    for j in range(NEED):
        tiles = []
        for q in range(8):
            lower, weight = lower_ref[pos, q] - base, weight_ref[pos, q]
            tiles.append(jnp.where(lower == j, weight, 0.0) + jnp.where(lower + 1 == j, 1.0 - weight, 0.0))
        row = [jnp.where(lane, tiles[2 * t], tiles[2 * t + 1]) for t in range(4)]
        coef.append(row[:2] + [row[2] * flip, row[3] * flip])
    field = [[None] * 4, [None] * 4]
    for j in range(NEED):
        for c in range(2):
            rows = slice(128 * j + 64 * c, 128 * j + 64 * c + 64)
            for t in range(4):
                lanes = slice(128 * (t % 2), 128 * (t % 2) + 128)
                u, v = halves[0][rows, lanes], halves[1][rows, lanes]
                term = (u + v if t < 2 else u - v) * coef[j][t]
                field[c][t] = term if j == 0 else field[c][t] + term
    image = []
    for t in range(4):
        lanes = slice(128 * t, 128 * t + 128)
        image.append(field[0][t] * source_ref[f, :, 0, lanes] + field[1][t] * source_ref[f, :, 1, lanes])
    out_ref, image_ref = refs[:2] if f == 0 else refs[1:3]
    for t in range(4):
        lanes = slice(128 * t, 128 * t + 128)
        for c in range(2):
            out_ref[c, :, lanes] = field[c][t]
        if f == 0:
            image_ref[:, lanes] = image[t]
    if f == 0:
        return
    part_ref = refs[0]
    group = lax.broadcasted_iota(jnp.int32, (8, 128), 1) // 16
    for t in range(4):
        lanes = slice(128 * t, 128 * t + 128)
        total = (image[t] + part_ref[:, lanes]) * (1.0 / 8.0)
        cells = [total[8 * b : 8 * b + 8] for b in range(8)]
        for bit in (1, 2, 4):
            low = (group & bit) == 0
            new = [None] * 8
            for b in range(8):
                if b & bit:
                    continue
                x, y = cells[b], cells[b | bit]
                new[b] = jnp.where(low, x, pltpu.roll(y, 16 * bit, 1))
                new[b | bit] = jnp.where(low, pltpu.roll(x, 128 - 16 * bit, 1), y)
            cells = new
        for g in range(8):
            image_ref[8 * t + g] = cells[g]


def store_field(first_ref, second_ref, out_ref):
    for f, ref in enumerate((first_ref, second_ref)):
        for c in range(2):
            out_ref[f, :, c, :] = ref[c]


def sum_image(came_ref, out_ref):
    total = jnp.sum(came_ref[...], axis=0).T
    out_ref[0] = jnp.concatenate([total[16 * b : 16 * b + 16] for b in range(8)], axis=1)


VM = pl.BlockSpec(memory_space=pltpu.VMEM)
SM = pl.BlockSpec(memory_space=pltpu.SMEM)
HB = pl.BlockSpec(memory_space=pltpu.HBM)


def call(body, out, specs, scratch=(), f=None, grant=16):
    many = isinstance(out, (tuple, list))
    return pl.pallas_call(
        body if f is None else functools.partial(body, f),
        out_shape=out,
        in_specs=specs,
        out_specs=tuple(VM for _ in out) if many else VM,
        scratch_shapes=list(scratch),
        compiler_params=pltpu.CompilerParams(vmem_limit_bytes=grant * 2**20),
        interpret=INTERPRET,
    )


def shape(*dims):
    return jax.ShapeDtypeStruct(dims, F32)


def permute(values, chips, core=0):
    pairs = [(2 * x + c, 2 * ((x + chips) % 4) + (c + core) % 2) for x in range(4) for c in range(2)]
    return lax.ppermute(values, "pencil", pairs)


def whole(wave_field, source_field, omegas, velocities, lower_ref, blend_weight):
    pos = lax.axis_index("pencil").reshape(1)
    lower, weight = lower_ref[0], blend_weight[0]
    back, ahead = (jnp.asarray(t) for t in tables())
    own, other = call(
        forward_y,
        [shape(2, 64, N)] * 2,
        [SM, HB, HB],
        [pltpu.VMEM(wave_field.shape, F32), pltpu.VMEM(back.shape, BF), pltpu.SemaphoreType.DMA((2,))],
        grant=FIRST,
    )(pos, wave_field, back)
    other = permute(other, 0, 1)
    here, right, left, far0, far1, phase = [], [], [], [], [], []
    for f in range(2):
        here.append(jnp.stack([own[f], other[f]]))
        right.append(permute(here[f], 1))
        left.append(permute(here[f], 3))
    for f in range(2):
        phase.append(
            call(
                phases,
                [shape(2 * NEED, 2, QUART, HALF)] * 2 + [shape(2 * NEED, 2, 8, HALF)],
                [SM] * 4,
                [pltpu.VMEM((2, QUART, 128), F32)],
                f=f,
            )(pos, lower, omegas, velocities[0])
        )
        far0.append(permute(right[f][0], 1))
        far1.append(permute(left[f][1], 3))
    fields, images = [], []
    for f in range(2):
        mine, theirs = call(
            shift_x,
            [shape(NEED, 64, N)] * 2,
            [SM] + [VM] * 10,
            [pltpu.VMEM((2, HALF, N), F32)] * 2,
            f,
        )(pos, here[f], right[f], left[f], far0[f], far1[f], *phase[f], ahead, back)
        came = permute(theirs, 0, 1)
        field, image = call(
            inverse_y,
            [shape(2, 64, N), shape(64, N) if f == 0 else shape(32, 8, 128)],
            [SM] * 3 + [VM] * (4 + f),
            f=f,
        )(pos, lower, weight, source_field[0], ahead, mine, came, *images)
        fields.append(field)
        images.append(image)
    return finish(*fields, images[-1])


def finish(first, second, image):
    came = lax.all_to_all(image, "freq", 0, 0, tiled=True)
    field = call(store_field, shape(2, 64, 2, N), [VM] * 2)(first, second)
    image = call(sum_image, shape(1, 16, 64), [VM])(came)
    return field, jnp.transpose(image, (0, 2, 1))


def solution(mesh):
    placed = (
        P("freq", "pencil", None, None),
        P(None, "freq", "pencil", None, None),
        P("freq"),
        P(),
        P(),
        P(),
    )
    return jax.shard_map(
        whole,
        mesh=mesh,
        in_specs=placed,
        out_specs=(P("freq", "pencil", None, None), P(None, "pencil", "freq")),
        check_vma=False,
    )
```

time: 71.9 us -> 61.6 us (0.86)
  the two profiles are of different devices: /device:TPU:2 before, /device:TPU:1 now
where the time goes in v2:
time: 61.6 us; the launch traced here: 61.5 us
  starting transfers between devices  26.9 us (44%)
  Pallas kernels  17.6 us (29%)
  waiting for transfers between devices  14.8 us (24%)
  local copies, waits for them, and re-layouts  1.17 us (2%)
  between operations  0.84 us (1%)
    ppermute x11, starting transfers between devices, permute(): return lax.ppermute(values, 'pencil', pairs)  17.4 us
    all_to_all x1, starting transfers between devices, finish(): came = lax.all_to_all(image, 'freq', 0, 0, tiled=True)  9.5 us
    all_to_all x1, waiting for transfers between devices, finish(): came = lax.all_to_all(image, 'freq', 0, 0, tiled=True)  8.26 us
    ppermute x11, waiting for transfers between devices, permute(): return lax.ppermute(values, 'pencil', pairs)  6.59 us
    pallas_call x2, Pallas kernels, whole(): call(phases, [shape(2 * NEED, 2, QUART, HALF)] * 2 + [shape(2 * NEED, 2,...  4.98 us
    pallas_call x2, Pallas kernels, whole(): call(shift_x, [shape(NEED, 64, N)] * 2, [SM] + [VM] * 10, [pltpu.VMEM((2,...  4.87 us
    pallas_call x2, Pallas kernels, whole(): call(inverse_y, [shape(2, 64, N), shape(64, N) if f == 0 else shape(32, 8...  3.64 us
    pallas_call x1, Pallas kernels, whole(): call(forward_y, [shape(2, 64, N)] * 2, [SM, HB, HB], [pltpu.VMEM(wave_fie...  2.47 us
  transfers between devices with their start and end apart: 12, of which 5 were waited for; matrix products, arithmetic and copies ran while one was open for 2% of the time, Pallas kernels for 20%

profile of v2, /device:TPU:1, one launch (start us, length us, event | category | flops | bytes accessed | tf_op | source)
XLA Modules:
  0.0 61.5 jit_solution(8348922603260399142)
XLA Ops:
  0.6 2.5 %shard_map.95 = (f32[2,64,512]{2,1,0:T(8,128)}, f32[2,64,512]{2,1,0:T(8,128)}) custom-call(s32[1]{0:T(128)} %bitcast.pos_ref, f32[2,64,2,512]{3,2,1,0:T(2,128)} %wave_hbm.1, bf16[2,2,256,256]{3,2,1,0:T(8,128)(2,1)} %constant.8.clone.table_hbm.b_ref), custom_call_target="tpu_custom_call" | custom-call | tf_op jit(solution)/shard_map/pallas_call | solution.py:289
  3.1 3.3 %collective-permute-start = (f32[2,64,512]{2,1,0:T(8,128)}, f32[2,64,512]{2,1,0:T(8,128)S(1)}, u32[]{:S(2)}, u32[]{:S(2)}) collective-permute-start(f32[2,64,512]{2,1,0:T(8,128)} %get-tuple-element.19), channel_id=1, source_target_pairs={{0,1},{1,0},{2,3},{3,2},{4,5},{5,4},{6,7},{7,6},{8,9},{9,8},{10,11... | collective-permute-start | bytes 786440 | tf_op jit(solution)/shard_map/ppermute | solution.py:282
  6.4 0.0 copy-start.3
  6.4 0.0 copy-start.5
  6.4 0.0 copy-start.6
  6.4 0.0 copy-start
  6.4 0.0 copy-start.1
  6.4 1.1 %fusion = (f32[1,64,512]{2,1,0:T(8,128)S(1)}, f32[1,64,512]{2,1,0:T(8,128)S(1)}) fusion(f32[2,64,512]{2,1,0:T(8,128)} %get-tuple-element.18), kind=kLoop, calls=%fused_computation.6 | loop fusion | bytes 524288 | tf_op jit(solution)/shard_map/slice | solution.py:299
  7.5 0.3 collective-permute-done
  7.8 0.1 collective-permute-start.1
  7.9 2.7 %collective-permute-start.2 = (f32[2,64,512]{2,1,0:T(8,128)S(1)}, f32[2,64,512]{2,1,0:T(8,128)S(1)}, u32[]{:S(2)}, u32[]{:S(2)}) collective-permute-start(f32[2,64,512]{2,1,0:T(8,128)S(1)} %pad_maximum_fusion.here_ref), channel_id=1, source_target_pairs={{0,6},{1,7},{2,0},{3,1},{4,2},{5,3},{6,4},{7,5},{8,14},{9,15},{10,... | collective-permute-start | bytes 786440 | tf_op jit(solution)/shard_map/ppermute | solution.py:282
  10.6 0.1 collective-permute-start.6
  10.7 2.7 %collective-permute-start.7 = (f32[2,64,512]{2,1,0:T(8,128)S(1)}, f32[2,64,512]{2,1,0:T(8,128)S(1)}, u32[]{:S(2)}, u32[]{:S(2)}) collective-permute-start(f32[2,64,512]{2,1,0:T(8,128)S(1)} %pad_maximum_fusion.1.here_ref), channel_id=1, source_target_pairs={{0,6},{1,7},{2,0},{3,1},{4,2},{5,3},{6,4},{7,5},{8,14},{9,15},{10,... | collective-permute-start | bytes 786440 | tf_op jit(solution)/shard_map/ppermute | solution.py:282
  13.3 3.2 %collective-permute-done.1.right_ref = f32[2,64,512]{2,1,0:T(8,128)S(1)} collective-permute-done((f32[2,64,512]{2,1,0:T(8,128)S(1)}, f32[2,64,512]{2,1,0:T(8,128)S(1)}, u32[]{:S(2)}, u32[]{:S(2)}) %collective-permute-start.1) | collective-permute-done | bytes 262176 | tf_op jit(solution)/shard_map/ppermute | solution.py:282
  16.6 0.1 collective-permute-start.3
  16.7 0.0 collective-permute-done.2.left_ref
  16.7 2.7 %collective-permute-start.4 = (f32[64,512]{1,0:T(8,128)S(1)}, f32[64,512]{1,0:T(8,128)S(1)}, u32[]{:S(2)}, u32[]{:S(2)}) collective-permute-start(f32[64,512]{1,0:T(8,128)S(1)} %slice_bitcast_fusion.2), channel_id=1, source_target_pairs={{0,6},{1,7},{2,0},{3,1},{4,2},{5,3},{6,4},{7,5},{8,14},{9,15},{10,... | collective-permute-start | bytes 393224 | tf_op jit(solution)/shard_map/ppermute | solution.py:282
  19.5 2.8 %collective-permute-done.6.right_ref = f32[2,64,512]{2,1,0:T(8,128)S(1)} collective-permute-done((f32[2,64,512]{2,1,0:T(8,128)S(1)}, f32[2,64,512]{2,1,0:T(8,128)S(1)}, u32[]{:S(2)}, u32[]{:S(2)}) %collective-permute-start.6) | collective-permute-done | bytes 262176 | tf_op jit(solution)/shard_map/ppermute | solution.py:282
  22.2 0.1 collective-permute-start.8
  22.3 0.0 collective-permute-done.7.left_ref
  22.3 2.7 %collective-permute-start.9 = (f32[64,512]{1,0:T(8,128)S(1)}, f32[64,512]{1,0:T(8,128)S(1)}, u32[]{:S(2)}, u32[]{:S(2)}) collective-permute-start(f32[64,512]{1,0:T(8,128)S(1)} %slice_bitcast_fusion), channel_id=1, source_target_pairs={{0,6},{1,7},{2,0},{3,1},{4,2},{5,3},{6,4},{7,5},{8,14},{9,15},{10,... | collective-permute-start | bytes 393224 | tf_op jit(solution)/shard_map/ppermute | solution.py:282
  25.1 0.0 copy-done.3
  25.1 0.0 copy-done.5
  25.1 0.0 copy-done.6
  25.1 2.5 %shard_map.96 = (f32[6,2,128,256]{3,2,1,0:T(8,128)S(1)}, f32[6,2,128,256]{3,2,1,0:T(8,128)S(1)}, f32[6,2,8,256]{3,2,1,0:T(8,128)S(1)}) custom-call(s32[1]{0:T(128)} %bitcast.pos_ref, s32[8,8]{1,0:T(8,128)S(1)} %bitcast.16, f32[2]{0:T(128)S(1)} %copy-done.5, f32[6]{0:T(128)S(1)} %bitcast.22), custom_call_target="tpu_custom_call" | custom-call | tf_op jit(solution)/shard_map/pallas_call | solution.py:304
  27.6 2.5 %shard_map.99 = (f32[6,2,128,256]{3,2,1,0:T(8,128)S(1)}, f32[6,2,128,256]{3,2,1,0:T(8,128)S(1)}, f32[6,2,8,256]{3,2,1,0:T(8,128)S(1)}) custom-call(s32[1]{0:T(128)} %bitcast.pos_ref, s32[8,8]{1,0:T(8,128)S(1)} %bitcast.17, f32[2]{0:T(128)S(1)} %copy-done.5, f32[6]{0:T(128)S(1)} %bitcast.23), custom_call_target="tpu_custom_call" | custom-call | tf_op jit(solution)/shard_map/pallas_call | solution.py:304
  30.1 0.0 collective-permute-done.3.far0_ref
  30.1 0.0 collective-permute-done.4.far1_ref
  30.1 0.0 copy-done
  30.1 0.0 copy-done.1
  30.1 2.4 %shard_map.97 = (f32[3,64,512]{2,1,0:T(8,128)S(1)}, f32[3,64,512]{2,1,0:T(8,128)S(1)}) custom-call(s32[1]{0:T(128)} %bitcast.pos_ref, f32[2,64,512]{2,1,0:T(8,128)S(1)} %pad_maximum_fusion.here_ref, f32[2,64,512]{2,1,0:T(8,128)S(1)} %collective-permute-done.1.right_ref, f32[2,64,512]{2,1,0:T(8,128)S(1)} %collective-permute-done.2.left_ref, ...), custom_call_target="tpu_custom_call" | custom-call | tf_op jit(solution)/shard_map/pallas_call | solution.py:316
  32.5 2.9 %collective-permute-start.5 = (f32[3,64,512]{2,1,0:T(8,128)S(1)}, f32[3,64,512]{2,1,0:T(8,128)S(1)}, u32[]{:S(2)}, u32[]{:S(2)}) collective-permute-start(f32[3,64,512]{2,1,0:T(8,128)S(1)} %get-tuple-element.24), channel_id=1, source_target_pairs={{0,1},{1,0},{2,3},{3,2},{4,5},{5,4},{6,7},{7,6},{8,9},{9,8},{10,11... | collective-permute-start | bytes 1179656 | tf_op jit(solution)/shard_map/ppermute | solution.py:282
  35.4 0.0 collective-permute-done.8.far0_ref
  35.4 0.0 collective-permute-done.9.far1_ref
  35.4 0.0 copy-start.2
  35.4 0.0 copy-start.4
  35.4 2.5 %shard_map.100 = (f32[3,64,512]{2,1,0:T(8,128)S(1)}, f32[3,64,512]{2,1,0:T(8,128)S(1)}) custom-call(s32[1]{0:T(128)} %bitcast.pos_ref, f32[2,64,512]{2,1,0:T(8,128)S(1)} %pad_maximum_fusion.1.here_ref, f32[2,64,512]{2,1,0:T(8,128)S(1)} %collective-permute-done.6.right_ref, f32[2,64,512]{2,1,0:T(8,128)S(1)} %collective-permute-done.7.left_ref, ...), custom_call_target="tpu_custom_call" | custom-call | tf_op jit(solution)/shard_map/pallas_call | solution.py:316
  37.9 0.1 collective-permute-start.10
  38.0 0.0 collective-permute-done.5.came_ref
  38.0 0.0 copy-done.2
  38.0 0.0 copy-done.4
  38.1 1.4 %shard_map.98 = (f32[2,64,512]{2,1,0:T(8,128)S(1)}, f32[64,512]{1,0:T(8,128)S(1)}) custom-call(s32[1]{0:T(128)} %bitcast.pos_ref, s32[8,8]{1,0:T(8,128)S(1)} %bitcast.18, f32[8,8]{1,0:T(8,128)S(1)} %bitcast.20, f32[2,64,2,512]{3,2,1,0:T(2,128)S(1)} %bitcast.14, bf16[2,2,256,256]{3,2,1,0:T(8,128)(2,1)S(1)} %copy-done, ...), custom_call_target="tpu_custom_call" | custom-call | tf_op jit(solution)/shard_map/pallas_call | solution.py:324
  39.4 0.3 collective-permute-done.10.came_ref
  39.7 2.3 %shard_map.101 = (f32[2,64,512]{2,1,0:T(8,128)S(1)}, f32[32,8,128]{2,1,0:T(8,128)}) custom-call(s32[1]{0:T(128)} %bitcast.pos_ref, s32[8,8]{1,0:T(8,128)S(1)} %bitcast.19, f32[8,8]{1,0:T(8,128)S(1)} %bitcast.21, f32[2,64,2,512]{3,2,1,0:T(2,128)S(1)} %bitcast.15, bf16[2,2,256,256]{3,2,1,0:T(8,128)(2,1)S(1)} %copy-done, ...), custom_call_target="tpu_custom_call" | custom-call | tf_op jit(solution)/shard_map/pallas_call | solution.py:324
  42.0 9.5 %all-to-all-start = ((f32[32,8,128]{2,1,0:T(8,128)}), f32[32,8,128]{2,1,0:T(8,128)S(1)}, u32[]{:S(2)}, u32[]{:S(2)}) async-start(f32[32,8,128]{2,1,0:T(8,128)} %get-tuple-element.33), calls=%async_computation | async-start | bytes 262144 | tf_op jit(solution)/shard_map/all_to_all | solution.py:336
  51.5 0.9 %shard_map.102 = f32[2,64,2,512]{3,2,1,0:T(2,128)} custom-call(f32[2,64,512]{2,1,0:T(8,128)S(1)} %get-tuple-element.25.first_ref, f32[2,64,512]{2,1,0:T(8,128)S(1)} %get-tuple-element.32.second_ref), custom_call_target="tpu_custom_call" | custom-call | tf_op jit(solution)/shard_map/pallas_call | solution.py:337
  52.4 8.3 %all-to-all-done.came_ref = f32[32,8,128]{2,1,0:T(8,128)S(1)} async-done(((f32[32,8,128]{2,1,0:T(8,128)}), f32[32,8,128]{2,1,0:T(8,128)S(1)}, u32[]{:S(2)}, u32[]{:S(2)}) %all-to-all-start) | async-done | bytes 131104 | tf_op jit(solution)/shard_map/all_to_all | solution.py:336
  60.7 0.8 %shard_map.103 = f32[1,16,64]{2,1,0:T(8,128)} custom-call(f32[32,8,128]{2,1,0:T(8,128)S(1)} %all-to-all-done.came_ref), custom_call_target="tpu_custom_call" | custom-call | tf_op jit(solution)/shard_map/pallas_call | solution.py:338
  (7 shorter events, 0.1 us)
Async XLA Ops:
  3.1 4.7 %collective-permute-start = (f32[2,64,512]{2,1,0:T(8,128)}, f32[2,64,512]{2,1,0:T(8,128)S(1)}, u32[]{:S(2)}, u32[]{:S(2)}) collective-permute-start(f32[2,64,512]{2,1,0:T(8,128)} %get-tuple-element.19), channel_id=1, source_target_pairs={{0,1},{1,0},{2,3},{3,2},{4,5},{5,4},{6,7},{7,6},{8,9},{9,8},{10,11... | collective-permute-start | bytes 786440 | tf_op jit(solution)/shard_map/ppermute | solution.py:282
  6.4 18.7 %copy-start.3 = (s32[1,8,8]{2,1,0:T(8,128)S(1)}, s32[1,8,8]{2,1,0:T(8,128)}, u32[]{:S(2)}) copy-start(s32[1,8,8]{2,1,0:T(8,128)} %param.12) | copy-start | bytes 772
  6.4 18.7 %copy-start.5 = (f32[2]{0:T(128)S(1)}, f32[2]{0:T(128)}, u32[]{:S(2)}) copy-start(f32[2]{0:T(128)} %omega_ref.3) | copy-start | bytes 28
  6.4 18.7 %copy-start.6 = (f32[1,6]{1,0:T(1,128)S(1)}, f32[1,6]{1,0:T(1,128)}, u32[]{:S(2)}) copy-start(f32[1,6]{1,0:T(1,128)} %param.11) | copy-start | bytes 76
  6.4 23.7 %copy-start = (bf16[2,2,256,256]{3,2,1,0:T(8,128)(2,1)S(1)}, bf16[2,2,256,256]{3,2,1,0:T(8,128)(2,1)}, u32[]{:S(2)}) copy-start(bf16[2,2,256,256]{3,2,1,0:T(8,128)(2,1)} %constant.9.clone.a_ref.table_ref) | copy-start | bytes 1572868
  6.4 23.7 %copy-start.1 = (bf16[2,2,256,256]{3,2,1,0:T(8,128)(2,1)S(1)}, bf16[2,2,256,256]{3,2,1,0:T(8,128)(2,1)}, u32[]{:S(2)}) copy-start(bf16[2,2,256,256]{3,2,1,0:T(8,128)(2,1)} %constant.8.clone.table_hbm.b_ref) | copy-start | bytes 1572868
  7.8 8.8 %collective-permute-start.1 = (f32[2,64,512]{2,1,0:T(8,128)S(1)}, f32[2,64,512]{2,1,0:T(8,128)S(1)}, u32[]{:S(2)}, u32[]{:S(2)}) collective-permute-start(f32[2,64,512]{2,1,0:T(8,128)S(1)} %pad_maximum_fusion.here_ref), channel_id=1, source_target_pairs={{0,2},{1,3},{2,4},{3,5},{4,6},{5,7},{6,0},{7,1},{8,10},{9,11},{10,... | collective-permute-start | bytes 786440 | tf_op jit(solution)/shard_map/ppermute | solution.py:282
  7.9 8.8 %collective-permute-start.2 = (f32[2,64,512]{2,1,0:T(8,128)S(1)}, f32[2,64,512]{2,1,0:T(8,128)S(1)}, u32[]{:S(2)}, u32[]{:S(2)}) collective-permute-start(f32[2,64,512]{2,1,0:T(8,128)S(1)} %pad_maximum_fusion.here_ref), channel_id=1, source_target_pairs={{0,6},{1,7},{2,0},{3,1},{4,2},{5,3},{6,4},{7,5},{8,14},{9,15},{10,... | collective-permute-start | bytes 786440 | tf_op jit(solution)/shard_map/ppermute | solution.py:282
  10.6 11.6 %collective-permute-start.6 = (f32[2,64,512]{2,1,0:T(8,128)S(1)}, f32[2,64,512]{2,1,0:T(8,128)S(1)}, u32[]{:S(2)}, u32[]{:S(2)}) collective-permute-start(f32[2,64,512]{2,1,0:T(8,128)S(1)} %pad_maximum_fusion.1.here_ref), channel_id=1, source_target_pairs={{0,2},{1,3},{2,4},{3,5},{4,6},{5,7},{6,0},{7,1},{8,10},{9,11},{10,... | collective-permute-start | bytes 786440 | tf_op jit(solution)/shard_map/ppermute | solution.py:282
  10.7 11.6 %collective-permute-start.7 = (f32[2,64,512]{2,1,0:T(8,128)S(1)}, f32[2,64,512]{2,1,0:T(8,128)S(1)}, u32[]{:S(2)}, u32[]{:S(2)}) collective-permute-start(f32[2,64,512]{2,1,0:T(8,128)S(1)} %pad_maximum_fusion.1.here_ref), channel_id=1, source_target_pairs={{0,6},{1,7},{2,0},{3,1},{4,2},{5,3},{6,4},{7,5},{8,14},{9,15},{10,... | collective-permute-start | bytes 786440 | tf_op jit(solution)/shard_map/ppermute | solution.py:282
  16.6 13.5 %collective-permute-start.3 = (f32[64,512]{1,0:T(8,128)S(1)}, f32[64,512]{1,0:T(8,128)S(1)}, u32[]{:S(2)}, u32[]{:S(2)}) collective-permute-start(f32[64,512]{1,0:T(8,128)S(1)} %slice_bitcast_fusion.3), channel_id=1, source_target_pairs={{0,2},{1,3},{2,4},{3,5},{4,6},{5,7},{6,0},{7,1},{8,10},{9,11},{10,... | collective-permute-start | bytes 393224 | tf_op jit(solution)/shard_map/ppermute | solution.py:282
  16.7 13.4 %collective-permute-start.4 = (f32[64,512]{1,0:T(8,128)S(1)}, f32[64,512]{1,0:T(8,128)S(1)}, u32[]{:S(2)}, u32[]{:S(2)}) collective-permute-start(f32[64,512]{1,0:T(8,128)S(1)} %slice_bitcast_fusion.2), channel_id=1, source_target_pairs={{0,6},{1,7},{2,0},{3,1},{4,2},{5,3},{6,4},{7,5},{8,14},{9,15},{10,... | collective-permute-start | bytes 393224 | tf_op jit(solution)/shard_map/ppermute | solution.py:282
  22.2 13.2 %collective-permute-start.8 = (f32[64,512]{1,0:T(8,128)S(1)}, f32[64,512]{1,0:T(8,128)S(1)}, u32[]{:S(2)}, u32[]{:S(2)}) collective-permute-start(f32[64,512]{1,0:T(8,128)S(1)} %slice_bitcast_fusion.1), channel_id=1, source_target_pairs={{0,2},{1,3},{2,4},{3,5},{4,6},{5,7},{6,0},{7,1},{8,10},{9,11},{10,... | collective-permute-start | bytes 393224 | tf_op jit(solution)/shard_map/ppermute | solution.py:282
  22.3 13.1 %collective-permute-start.9 = (f32[64,512]{1,0:T(8,128)S(1)}, f32[64,512]{1,0:T(8,128)S(1)}, u32[]{:S(2)}, u32[]{:S(2)}) collective-permute-start(f32[64,512]{1,0:T(8,128)S(1)} %slice_bitcast_fusion), channel_id=1, source_target_pairs={{0,6},{1,7},{2,0},{3,1},{4,2},{5,3},{6,4},{7,5},{8,14},{9,15},{10,... | collective-permute-start | bytes 393224 | tf_op jit(solution)/shard_map/ppermute | solution.py:282
  32.5 5.5 %collective-permute-start.5 = (f32[3,64,512]{2,1,0:T(8,128)S(1)}, f32[3,64,512]{2,1,0:T(8,128)S(1)}, u32[]{:S(2)}, u32[]{:S(2)}) collective-permute-start(f32[3,64,512]{2,1,0:T(8,128)S(1)} %get-tuple-element.24), channel_id=1, source_target_pairs={{0,1},{1,0},{2,3},{3,2},{4,5},{5,4},{6,7},{7,6},{8,9},{9,8},{10,11... | collective-permute-start | bytes 1179656 | tf_op jit(solution)/shard_map/ppermute | solution.py:282
  35.4 2.6 %copy-start.2 = (f32[1,2,64,2,512]{4,3,2,1,0:T(2,128)S(1)}, f32[1,2,64,2,512]{4,3,2,1,0:T(2,128)}, u32[]{:S(2)}) copy-start(f32[1,2,64,2,512]{4,3,2,1,0:T(2,128)} %param.9) | copy-start | bytes 1572868
  35.4 2.6 %copy-start.4 = (f32[1,8,8]{2,1,0:T(8,128)S(1)}, f32[1,8,8]{2,1,0:T(8,128)}, u32[]{:S(2)}) copy-start(f32[1,8,8]{2,1,0:T(8,128)} %param.13) | copy-start | bytes 772
  37.9 1.8 %collective-permute-start.10 = (f32[3,64,512]{2,1,0:T(8,128)S(1)}, f32[3,64,512]{2,1,0:T(8,128)S(1)}, u32[]{:S(2)}, u32[]{:S(2)}) collective-permute-start(f32[3,64,512]{2,1,0:T(8,128)S(1)} %get-tuple-element.30), channel_id=1, source_target_pairs={{0,1},{1,0},{2,3},{3,2},{4,5},{5,4},{6,7},{7,6},{8,9},{9,8},{10,11... | collective-permute-start | bytes 1179656 | tf_op jit(solution)/shard_map/ppermute | solution.py:282
  42.0 18.7 %all-to-all-start = ((f32[32,8,128]{2,1,0:T(8,128)}), f32[32,8,128]{2,1,0:T(8,128)S(1)}, u32[]{:S(2)}, u32[]{:S(2)}) async-start(f32[32,8,128]{2,1,0:T(8,128)} %get-tuple-element.33), calls=%async_computation | async-start | bytes 262144 | tf_op jit(solution)/shard_map/all_to_all | solution.py:336
